TPU v7x, 32 devices: a whole 2x2x4 slice. The times are simulated.
32 devices in a mesh: dp: 8 (over z, y), mp: 4 (over x, core).
Axes of the slice: x: 2, y: 2, z: 4, core: 2. Of those that a mesh axis runs over, the one named last changes fastest.
Arguments:
- block_input: float32 [4096, 768], P(('dp', 'mp')), may hold values from -54 to 54
- out_cotangent: float32 [4096, 768], P(('dp', 'mp')), may hold values from -6 to 6
- gain_attend: float32 [768], P('dp'), may hold values from 0.5 to 1.5
- weight_triple: float32 [3, 768, 768], P(None, 'dp', 'mp'), may hold values from -4 to 4
- weight_merge: float32 [768, 768], P('mp', 'dp'), may hold values from -0.875 to 0.875
- gain_feed: float32 [768], P('dp'), may hold values from 0.5 to 1.5
- weight_expand: float32 [2, 768, 1152], P(None, 'dp', 'mp'), may hold values from -0.21875 to 0.21875
- weight_reduce: float32 [1152, 768], P('mp', 'dp'), may hold values from -0.1875 to 0.1875
- mean_attend: float32 [768], P('dp'), may hold values from -40 to 40
- mean_triple: float32 [3, 768, 768], P(None, 'dp', 'mp'), may hold values from -40 to 40
- mean_merge: float32 [768, 768], P('mp', 'dp'), may hold values from -40 to 40
- mean_feed: float32 [768], P('dp'), may hold values from -40 to 40
- mean_expand: float32 [2, 768, 1152], P(None, 'dp', 'mp'), may hold values from -40 to 40
- mean_reduce: float32 [1152, 768], P('mp', 'dp'), may hold values from -40 to 40
- square_attend: float32 [768], P('dp'), may hold values from 1.3653333 to 13.653334
- square_triple: float32 [3, 768, 768], P(None, 'dp', 'mp'), may hold values from 1.3653333 to 13.653334
- square_merge: float32 [768, 768], P('mp', 'dp'), may hold values from 1.3653333 to 13.653334
- square_feed: float32 [768], P('dp'), may hold values from 1.3653333 to 13.653334
- square_expand: float32 [2, 768, 1152], P(None, 'dp', 'mp'), may hold values from 1.3653333 to 13.653334
- square_reduce: float32 [1152, 768], P('mp', 'dp'), may hold values from 1.3653333 to 13.653334
Outputs:
- block_output: float32 [4096, 768], P(('dp', 'mp'))
- input_grad: float32 [4096, 768], P(('dp', 'mp'))
- grad_attend: float32 [768], P('dp')
- grad_triple: float32 [3, 768, 768], P(None, 'dp', 'mp')
- grad_merge: float32 [768, 768], P('mp', 'dp')
- grad_feed: float32 [768], P('dp')
- grad_expand: float32 [2, 768, 1152], P(None, 'dp', 'mp')
- grad_reduce: float32 [1152, 768], P('mp', 'dp')
- fresh_attend: float32 [768], P('dp')
- fresh_triple: float32 [3, 768, 768], P(None, 'dp', 'mp')
- fresh_merge: float32 [768, 768], P('mp', 'dp')
- fresh_feed: float32 [768], P('dp')
- fresh_expand: float32 [2, 768, 1152], P(None, 'dp', 'mp')
- fresh_reduce: float32 [1152, 768], P('mp', 'dp')
- first_attend: float32 [768], P('dp')
- first_triple: float32 [3, 768, 768], P(None, 'dp', 'mp')
- first_merge: float32 [768, 768], P('mp', 'dp')
- first_feed: float32 [768], P('dp')
- first_expand: float32 [2, 768, 1152], P(None, 'dp', 'mp')
- first_reduce: float32 [1152, 768], P('mp', 'dp')
- second_attend: float32 [768], P('dp')
- second_triple: float32 [3, 768, 768], P(None, 'dp', 'mp')
- second_merge: float32 [768, 768], P('mp', 'dp')
- second_feed: float32 [768], P('dp')
- second_expand: float32 [2, 768, 1152], P(None, 'dp', 'mp')
- second_reduce: float32 [1152, 768], P('mp', 'dp')
All inputs are finite; a program needn't handle non-finite values.
Results may differ from a plain program's by a relative error of at most 0.017.
Values may be sent and summed in bfloat16 or wider, within the bound.
No kernel may reach another device: no remote copies, remote signals or barrier semaphores. Data moves between devices by JAX's collectives and lax.ppermute only.
A program may use at most 64 MiB of HBM per device.

v0:
```python
import math

import jax
import jax.numpy as jnp
import numpy as np
from jax import lax
from jax.experimental import pallas as pl
from jax.experimental.pallas import tpu as pltpu
from jax.sharding import PartitionSpec as P


HD = 64
WINDOW = 128
HALF = WINDOW // 2
TILE = 128
LANES = 128

NORM_EPS = 1e-05
ROPE_BASE = 10000.0
BETA_FIRST = 0.9
BETA_SECOND = 0.999
ADAM_EPS = 1e-08
DECAY = 0.01
RATE_MATRIX = 0.02
RATE_GAIN = 0.2
STEP_COUNT = 3.0
MASKED = -1e30

INTERPRET = False
F32 = jnp.float32
BF16 = jnp.bfloat16


def run_kernel(body, outs, args, scalars=0, scratch=(), limit=24, final=False):
    in_specs = [pl.BlockSpec(memory_space=pltpu.SMEM)] * scalars
    in_specs += [pl.BlockSpec(memory_space=pltpu.VMEM)] * (len(args) - scalars)
    out_shape = [jax.ShapeDtypeStruct(shape, kind) for shape, kind in outs]
    if not INTERPRET:
        args = args[:scalars] + tuple(
            pltpu.with_memory_space_constraint(item, pltpu.VMEM) for item in args[scalars:]
        )
        if not final:
            out_shape = [pltpu.VMEM(shape, kind) for shape, kind in outs]
    return pl.pallas_call(
        body,
        out_shape=out_shape,
        in_specs=in_specs,
        out_specs=[pl.BlockSpec(memory_space=pltpu.VMEM)] * len(outs),
        scratch_shapes=list(scratch),
        interpret=INTERPRET,
        compiler_params=pltpu.CompilerParams(vmem_limit_bytes=limit << 20),
    )(*args)


def dot_nn(left, right):
    return lax.dot_general(left, right, (((1,), (0,)), ((), ())), preferred_element_type=F32)


def dot_nt(left, right):
    return lax.dot_general(left, right, (((1,), (1,)), ((), ())), preferred_element_type=F32)


def dot_tn(left, right):
    return lax.dot_general(left, right, (((0,), (0,)), ((), ())), preferred_element_type=F32)


def lane_iota(shape):
    return lax.broadcasted_iota(jnp.int32, shape, len(shape) - 1)


def shift(value, amount):
    return pltpu.roll(value, amount, 1)


def rope_tables(length):
    half = HD // 2
    freqs = np.power(np.float64(ROPE_BASE), -2.0 * np.arange(half) / HD)
    angles = np.arange(length)[:, None] * freqs[None, :]
    tile = LANES // half
    return (
        np.tile(np.cos(angles), (1, tile)).astype(np.float32),
        np.tile(np.sin(angles), (1, tile)).astype(np.float32),
    )


def turn(value, cosine, sine, back):
    lanes = lane_iota(value.shape)
    first = (lanes % HD) < HD // 2
    ahead = shift(value, LANES - HD // 2)
    behind = shift(value, HD // 2)
    if back:
        other = jnp.where(first, ahead, -behind)
    else:
        other = jnp.where(first, -ahead, behind)
    return value * cosine + other * sine


def gelu_parts(value):
    normal_share = 0.5 * (1.0 + lax.erf(value * (1.0 / math.sqrt(2.0))))
    density = jnp.exp(-0.5 * value * value) * (1.0 / math.sqrt(2.0 * math.pi))
    return (value * normal_share, normal_share + value * density)


def row_stats(rows):
    center = rows - jnp.mean(rows, axis=-1, keepdims=True)
    scale = lax.rsqrt(jnp.mean(center * center, axis=-1, keepdims=True) + NORM_EPS)
    return center * scale, scale


def scaled_back(scaled, normed, scale):
    return scale * (
        scaled
        - jnp.mean(scaled, axis=-1, keepdims=True)
        - normed * jnp.mean(scaled * normed, axis=-1, keepdims=True)
    )


def at_block(offsets, index, size):
    return pl.ds(pl.multiple_of(offsets[index], size), size)


def tile_mask(start, length):
    row = lax.broadcasted_iota(jnp.int32, (TILE, TILE + WINDOW), 0)
    col = lax.broadcasted_iota(jnp.int32, (TILE, TILE + WINDOW), 1)
    ahead = col - row
    key = col + (start - HALF)
    return (ahead >= 0) & (ahead <= WINDOW) & (key >= 0) & (key < length)


def low_high():
    lanes = lane_iota((1, LANES))
    low = (lanes < HD).astype(F32)
    return low.astype(BF16), (1.0 - low).astype(BF16)


def fill_padded(target, value, length):
    target[0:HALF, :] = jnp.zeros((HALF, LANES), target.dtype)
    target[HALF + length : length + WINDOW, :] = jnp.zeros((HALF, LANES), target.dtype)
    target[HALF : HALF + length, :] = value


def prepare_kernel(places, spots, rows_ref, cot_ref, out_ref):
    width = rows_ref.shape[1]
    normed, _ = row_stats(rows_ref[...])
    out_ref[:, :width] = normed.astype(BF16)
    out_ref[:, width:] = cot_ref[...].astype(BF16)


def make_attend(length, width, rows, chunks):
    scale = 1.0 / math.sqrt(HD)

    def body(places, spots, cos_ref, sin_ref, *refs):
        blocks, refs = refs[:4], refs[4:]
        parts, refs = refs[:chunks], refs[chunks:]
        normed, cot, weight, qkv, att, lse, keep, send = refs[:8]
        k_pad, k2_pad, v_pad, v2_pad, partial = refs[8:]
        deep = width // chunks
        for j in range(4):
            normed[at_block(places, j, rows), :] = blocks[j][:, :width]
            cot[at_block(places, j, rows), :] = blocks[j][:, width:]
        for s in range(chunks):
            weight[at_block(spots, s, deep), :] = parts[s][...]
        pre = dot_nn(normed[...], weight[:, : 5 * LANES])
        cosine, sine = cos_ref[...], sin_ref[...]
        lanes = lane_iota((length, LANES))
        is_low = lanes < HD
        for t in range(3):
            turned = turn(pre[:, t * LANES : (t + 1) * LANES], cosine, sine, False)
            qkv[:, t * LANES : (t + 1) * LANES] = turned.astype(BF16)
            if t == 1:
                fill_padded(k_pad, turned.astype(BF16), length)
            if t == 2:
                fill_padded(k2_pad, shift(turned, HD).astype(BF16), length)
        v_main = pre[:, 3 * LANES : 4 * LANES].astype(BF16)
        v_rest = jnp.where(is_low, pre[:, 4 * LANES : 5 * LANES], 0.0).astype(BF16)
        qkv[:, 3 * LANES : 4 * LANES] = v_main
        qkv[:, 4 * LANES : 5 * LANES] = v_rest
        fill_padded(v_pad, v_main, length)
        fill_padded(v2_pad, v_rest, length)
        low, high = low_high()
        tile_lanes = lane_iota((TILE, LANES))
        tile_low = tile_lanes < HD
        for t in range(length // TILE):
            span = slice(t * TILE, (t + 1) * TILE)
            window = slice(t * TILE, (t + 1) * TILE + WINDOW)
            mask = tile_mask(t * TILE, length)
            q_main, q_rest = qkv[span, 0:LANES], qkv[span, 2 * LANES : 3 * LANES]
            found, totals = [], []
            for q, k_ref, v_ref in (
                (q_main * low, k_pad, v_pad),
                (q_main * high, k_pad, v_pad),
                (q_rest * low, k2_pad, v2_pad),
            ):
                score = jnp.where(mask, dot_nt(q, k_ref[window, :]) * scale, MASKED)
                top = jnp.max(score, axis=-1, keepdims=True)
                total = top + jnp.log(jnp.sum(jnp.exp(score - top), axis=-1, keepdims=True))
                probs = jnp.exp(score - total).astype(BF16)
                found.append(dot_nn(probs, v_ref[window, :]))
                totals.append(total)
            main = jnp.where(tile_low, found[0], found[1])
            rest = shift(jnp.where(tile_low, found[2], 0.0), HD)
            att[span, 0:LANES] = rest.astype(BF16)
            att[span, LANES : 2 * LANES] = main.astype(BF16)
            lse[span, :] = jnp.where(
                tile_lanes == 0, totals[0], jnp.where(tile_lanes == 1, totals[1], totals[2])
            )
        partial[...] = dot_nt(att[...], weight[:, 4 * LANES :])
        for i, j in enumerate((0, 2)):
            keep[i] = partial[at_block(places, j, rows), :]
        for i, j in enumerate((1, 3)):
            send[i] = partial[at_block(places, j, rows), :].astype(BF16)

    return body


def core_sum_kernel(keep_ref, got_ref, mine_ref, send_ref):
    mine_ref[...] = keep_ref[0] + got_ref[0].astype(F32)
    send_ref[...] = (keep_ref[1] + got_ref[1].astype(F32)).astype(BF16)


def second_norm_kernel(rows_ref, mine_ref, got_ref, residual_ref, normed_ref):
    residual = rows_ref[...] + mine_ref[...] + got_ref[...].astype(F32)
    residual_ref[...] = residual
    normed, _ = row_stats(residual)
    normed_ref[...] = normed.astype(BF16)


def make_feed(length, width, rows, chunks):
    def body(places, spots, *refs):
        blocks, refs = refs[:4], refs[4:]
        cot, refs = refs[0], refs[1:]
        parts, refs = refs[:chunks], refs[chunks:]
        normed, d_all, inner_all, keep_s, send_s, keep_o, send_o = refs[:7]
        weight, partial = refs[7:]
        deep = width // chunks
        for j in range(4):
            normed[at_block(places, j, rows), :] = blocks[j][...]
        for s in range(chunks):
            weight[at_block(spots, s, deep), :] = parts[s][...]
        both = dot_nn(normed[...], weight[:, : 5 * LANES])
        d_inner = dot_nn(cot[...], weight[:, 4 * LANES :])
        lanes = lane_iota((length, LANES))
        valid = lanes < LANES // 4
        for t in range(3):
            if t < 2:
                gate = both[:, t * LANES : (t + 1) * LANES]
                up = both[:, (2 + t) * LANES : (3 + t) * LANES]
                slope_in = d_inner[:, (1 + t) * LANES : (2 + t) * LANES]
            else:
                gate = both[:, 4 * LANES : 5 * LANES]
                up = shift(gate, LANES - LANES // 4)
                slope_in = shift(d_inner[:, 0:LANES], LANES // 2)
            value, slope = gelu_parts(gate)
            inner = value * up
            d_gate = slope_in * up * slope
            d_up = slope_in * value
            if t < 2:
                inner_all[:, (1 + t) * LANES : (2 + t) * LANES] = inner.astype(BF16)
                d_all[:, t * LANES : (t + 1) * LANES] = d_gate.astype(BF16)
                d_all[:, (2 + t) * LANES : (3 + t) * LANES] = d_up.astype(BF16)
            else:
                inner_all[:, 0:LANES] = shift(
                    jnp.where(valid, inner, 0.0), LANES // 2
                ).astype(BF16)
                d_all[:, 4 * LANES : 5 * LANES] = jnp.where(
                    valid, d_gate, shift(jnp.where(valid, d_up, 0.0), LANES // 4)
                ).astype(BF16)
        partial[...] = dot_nt(d_all[...], weight[:, : 5 * LANES])
        for i, j in enumerate((0, 2)):
            keep_s[i] = partial[at_block(places, j, rows), :]
        for i, j in enumerate((1, 3)):
            send_s[i] = partial[at_block(places, j, rows), :].astype(BF16)
        partial[...] = dot_nt(inner_all[...], weight[:, 4 * LANES :])
        for i, j in enumerate((0, 2)):
            keep_o[i] = partial[at_block(places, j, rows), :]
        for i, j in enumerate((1, 3)):
            send_o[i] = partial[at_block(places, j, rows), :].astype(BF16)

    return body


def spread_chunks(grad, spots, outs, deep, chunks):
    if chunks == 1:
        outs[0][...] = grad[...]
        return
    group = outs[0].shape[0]
    for i in range(chunks // 2):
        mine, send = outs[2 * (i // group)], outs[2 * (i // group) + 1]
        mine[i % group] = grad[at_block(spots, 2 * i, deep), :]
        send[i % group] = grad[at_block(spots, 2 * i + 1, deep), :].astype(BF16)


def chunk_outs(chunks, deep, lanes, groups):
    if chunks == 1:
        return [((deep, lanes), F32)]
    shape = (chunks // 2 // groups, deep, lanes)
    return [(shape, F32), (shape, BF16)] * groups


def chunk_sum_kernel(mine_ref, got_ref, *outs):
    for i, out in enumerate(outs):
        out[...] = (mine_ref[i] + got_ref[i].astype(F32)).astype(out.dtype)


def spread_pairs(grad, spots, outs, deep, chunks):
    if chunks == 1:
        outs[0][...] = grad[...]
        return
    for i, out in enumerate(outs[:-2]):
        for side in range(2):
            out[side] = grad[at_block(spots, 2 * i + side, deep), :].astype(out.dtype)
    outs[-2][...] = grad[at_block(spots, chunks - 2, deep), :]
    outs[-1][...] = grad[at_block(spots, chunks - 1, deep), :].astype(BF16)


def pair_outs(chunks, deep, lanes):
    if chunks == 1:
        return [((deep, lanes), F32)]
    pairs = [((2, deep, lanes), BF16 if i else F32) for i in range(chunks // 2 - 1)]
    return pairs + [((deep, lanes), F32), ((deep, lanes), BF16)]


def near_sum_kernel(mine, got, out):
    out[...] = (mine[...] + got[...].astype(F32)).astype(out.dtype)


def pair_sum_kernel(*refs):
    parts, (mine, send) = refs[:-2], refs[-2:]
    for side, out in enumerate((mine, send)):
        total = parts[0][side]
        for part in parts[1:]:
            total = total + part[side].astype(F32)
        out[...] = total.astype(out.dtype)


def make_feed_grads(chunks):
    def body(spots, normed, cot, d_all, inner_all, *refs):
        outs, grad = refs[:-1], refs[-1]
        expand = dot_tn(normed[...], d_all[...])
        reduce = dot_tn(cot[...], inner_all[...])
        grad[:, : 4 * LANES] = expand[:, : 4 * LANES]
        grad[:, 4 * LANES : 5 * LANES] = expand[:, 4 * LANES :] + reduce[:, :LANES]
        grad[:, 5 * LANES :] = reduce[:, LANES:]
        spread_pairs(grad, spots, outs, grad.shape[0] // chunks, chunks)

    return body


def residual_back_kernel(cot_ref, residual_ref, mine_ref, got_ref, grad_ref, send_ref):
    normed, scale = row_stats(residual_ref[...])
    scaled = mine_ref[...] + got_ref[...].astype(F32)
    grad = cot_ref[...] + scaled_back(scaled, normed, scale)
    grad_ref[...] = grad
    send_ref[...] = grad.astype(BF16)


def make_attend_back(length, width, rows, chunks):
    scale = 1.0 / math.sqrt(HD)

    def body(places, spots, cos_ref, sin_ref, *refs):
        blocks, refs = refs[:4], refs[4:]
        normed, weight, qkv, att, lse = refs[:5]
        d_pre = refs[5]
        outs = refs[6:-11]
        resid, grad, k_pad, k2_pad, v_pad, v2_pad, da, dk, dk2, dv, dv2 = refs[-11:]
        for j in range(4):
            resid[at_block(places, j, rows), :] = blocks[j][...]
        back = dot_nn(resid[...], weight[:, 4 * LANES :])
        lanes = lane_iota((length, LANES))
        is_low = lanes < HD
        da[:, LANES:] = back[:, LANES:].astype(BF16)
        da[:, :LANES] = shift(jnp.where(is_low, 0.0, back[:, :LANES]), HD).astype(BF16)
        fill_padded(k_pad, qkv[:, LANES : 2 * LANES], length)
        fill_padded(
            k2_pad, shift(qkv[:, 2 * LANES : 3 * LANES].astype(F32), HD).astype(BF16), length
        )
        fill_padded(v_pad, qkv[:, 3 * LANES : 4 * LANES], length)
        fill_padded(v2_pad, qkv[:, 4 * LANES : 5 * LANES], length)
        for piece in (dk, dk2, dv, dv2):
            piece[...] = jnp.zeros_like(piece)
        low, high = low_high()
        tile_low = lane_iota((TILE, LANES)) < HD
        cosine, sine = cos_ref[...], sin_ref[...]
        for t in range(length // TILE):
            span = slice(t * TILE, (t + 1) * TILE)
            window = slice(t * TILE, (t + 1) * TILE + WINDOW)
            mask = tile_mask(t * TILE, length)
            q_main, q_rest = qkv[span, 0:LANES], qkv[span, 2 * LANES : 3 * LANES]
            da_main, da_rest = da[span, LANES:], da[span, :LANES]
            main = da_main.astype(F32) * att[span, LANES:].astype(F32)
            rest = da_rest.astype(F32) * shift(att[span, :LANES].astype(F32), HD)
            deltas = (
                jnp.sum(jnp.where(tile_low, main, 0.0), axis=-1, keepdims=True),
                jnp.sum(jnp.where(tile_low, 0.0, main), axis=-1, keepdims=True),
                jnp.sum(jnp.where(tile_low, rest, 0.0), axis=-1, keepdims=True),
            )
            d_query = []
            for h, (q, d, k_ref, v_ref, dk_ref, dv_ref) in enumerate(
                (
                    (q_main * low, da_main * low, k_pad, v_pad, dk, dv),
                    (q_main * high, da_main * high, k_pad, v_pad, dk, dv),
                    (q_rest * low, da_rest * low, k2_pad, v2_pad, dk2, dv2),
                )
            ):
                keys = k_ref[window, :]
                score = jnp.where(mask, dot_nt(q, keys) * scale, MASKED)
                probs = jnp.exp(score - lse[span, h : h + 1])
                d_probs = dot_nt(d, v_ref[window, :])
                d_score = (probs * (d_probs - deltas[h]) * scale).astype(BF16)
                d_query.append(dot_nn(d_score, keys))
                dk_ref[window, :] += dot_tn(d_score, q)
                dv_ref[window, :] += dot_tn(probs.astype(BF16), d)
            d_main = jnp.where(tile_low, d_query[0], d_query[1])
            d_pre[span, 0:LANES] = turn(d_main, cosine[span], sine[span], True).astype(BF16)
            grad[span, 0:LANES] = jnp.where(tile_low, d_query[2], 0.0)
        inside = slice(HALF, HALF + length)
        d_pre[:, LANES : 2 * LANES] = turn(dk[inside, :], cosine, sine, True).astype(BF16)
        rest = jnp.where(is_low, grad[0:length, 0:LANES], shift(dk2[inside, :], HD))
        d_pre[:, 2 * LANES : 3 * LANES] = turn(rest, cosine, sine, True).astype(BF16)
        d_pre[:, 3 * LANES : 4 * LANES] = dv[inside, :].astype(BF16)
        d_pre[:, 4 * LANES : 5 * LANES] = dv2[inside, :].astype(BF16)
        triple = dot_tn(normed[...], d_pre[...])
        merge = dot_tn(resid[...], att[...])
        grad[:, : 4 * LANES] = triple[:, : 4 * LANES]
        grad[:, 4 * LANES : 5 * LANES] = triple[:, 4 * LANES :] + merge[:, :LANES]
        grad[:, 5 * LANES :] = merge[:, LANES:]
        spread_chunks(grad, spots, outs, width // chunks, chunks)

    return body


def make_input_share(rows):
    def body(places, d_pre, weight, keep, send, partial):
        partial[...] = dot_nt(d_pre[...], weight[:, : 5 * LANES])
        for i, j in enumerate((0, 2)):
            keep[i] = partial[at_block(places, j, rows), :]
        for i, j in enumerate((1, 3)):
            send[i] = partial[at_block(places, j, rows), :].astype(BF16)

    return body


def finish_kernel(
    rows_ref, d_residual_ref, mine_ref, got_ref, residual_ref, out_mine, out_got, grad_ref, out_ref
):
    normed, scale = row_stats(rows_ref[...])
    scaled = mine_ref[...] + got_ref[...].astype(F32)
    grad_ref[...] = d_residual_ref[...] + scaled_back(scaled, normed, scale)
    out_ref[...] = residual_ref[...] + out_mine[...] + out_got[...].astype(F32)


def adam_step(weight, first, second, grad, rate):
    first_new = BETA_FIRST * first + (1.0 - BETA_FIRST) * grad
    second_new = BETA_SECOND * second + (1.0 - BETA_SECOND) * grad * grad
    first_hat = first_new / (1.0 - BETA_FIRST**STEP_COUNT)
    second_hat = second_new / (1.0 - BETA_SECOND**STEP_COUNT)
    fresh = weight - rate * (first_hat / (jnp.sqrt(second_hat) + ADAM_EPS) + DECAY * weight)
    return (fresh, first_new, second_new)


def column_of(row):
    count = row.shape[1]
    down = lax.broadcasted_iota(jnp.int32, (count, count), 0)
    along = lax.broadcasted_iota(jnp.int32, (count, count), 1)
    return jnp.sum(jnp.where(down == along, row, 0.0), axis=1, keepdims=True)


def row_of(column):
    count = column.shape[0]
    down = lax.broadcasted_iota(jnp.int32, (count, LANES), 0)
    along = lax.broadcasted_iota(jnp.int32, (count, LANES), 1)
    return jnp.sum(jnp.where(down == along, column, 0.0), axis=0, keepdims=True)


def rounded(value):
    return value.astype(BF16).astype(F32)


def pack_attend_kernel(gain_ref, triple_ref, merge_ref, out_ref):
    gain = column_of(rounded(gain_ref[...]))
    q, k, v = (rounded(triple_ref[c]) * gain for c in range(3))
    merge = merge_ref[...].T
    out_ref[...] = jnp.concatenate(
        [
            q[:, :LANES],
            k[:, :LANES],
            q[:, LANES:],
            k[:, LANES:],
            v[:, :LANES],
            v[:, LANES:],
            merge[:, LANES:],
            merge[:, :LANES],
        ],
        axis=1,
    ).astype(BF16)


def pack_feed_kernel(gain_ref, expand_ref, reduce_ref, out_ref):
    gain = column_of(rounded(gain_ref[...]))
    one, two = (rounded(expand_ref[c]) * gain for c in range(2))
    turned = reduce_ref[...].T
    wide = 2 * LANES
    spare = jnp.zeros((turned.shape[0], LANES // 4), F32)
    out_ref[...] = jnp.concatenate(
        [
            one[:, :wide],
            two[:, :wide],
            one[:, wide:],
            two[:, wide:],
            turned[:, wide:],
            spare,
            turned[:, :wide],
        ],
        axis=1,
    ).astype(BF16)


def total_of(parts):
    total = parts[0][...]
    for part in parts[1:]:
        total = total + part[...].astype(F32)
    return total


def adam_store(index, grad, rate, weight, first, second, grad_out, fresh_out, first_out, second_out):
    fresh, first_new, second_new = adam_step(weight[index], first[index], second[index], grad, rate)
    grad_out[index] = grad
    fresh_out[index] = fresh
    first_out[index] = first_new
    second_out[index] = second_new


def share_of(plain, weight):
    total = jnp.zeros((plain[0].shape[0], 1), F32)
    for c, grad in enumerate(plain):
        total = total + jnp.sum(grad * rounded(weight[c]), axis=1, keepdims=True)
    return row_of(total)


def attend_plain(pack):
    q = jnp.concatenate([pack[:, :LANES], pack[:, 2 * LANES : 2 * LANES + HD]], axis=1)
    k = jnp.concatenate([pack[:, LANES : 2 * LANES], pack[:, 2 * LANES + HD : 3 * LANES]], axis=1)
    v = jnp.concatenate([pack[:, 3 * LANES : 4 * LANES], pack[:, 4 * LANES : 4 * LANES + HD]], axis=1)
    return q, k, v


def make_share(count):
    def body(*refs):
        parts, (weight, other, out) = refs[:count], refs[count:]
        plain = attend_plain(total_of(parts))
        row = lax.broadcasted_iota(jnp.int32, (8, LANES), 0)
        out[...] = jnp.where(row == 0, share_of(plain, weight), other[...])

    return body


def make_adam_attend(count):
    def body(*refs):
        parts, refs = refs[:count], refs[count:]
        gain, refs = refs[0], refs[1:]
        triple, merge = refs[0::2], refs[1::2]
        pack = total_of(parts)
        scale = column_of(rounded(gain[...]))
        for c, grad in enumerate(attend_plain(pack)):
            adam_store(c, grad * scale, RATE_MATRIX, *triple)
        grad = jnp.concatenate([pack[:, 5 * LANES :], pack[:, 4 * LANES + HD : 5 * LANES]], axis=1)
        adam_store(Ellipsis, grad.T, RATE_MATRIX, *merge)

    return body


def make_adam_feed(count):
    def body(*refs):
        parts, refs = refs[:count], refs[count:]
        gain, share, refs = refs[0], refs[-1], refs[1:-1]
        expand, reduce = refs[0::2], refs[1::2]
        pack = total_of(parts)
        wide, part = 2 * LANES, LANES // 4
        rest = pack[:, 4 * LANES : 5 * LANES]
        plain = (
            jnp.concatenate([pack[:, :wide], rest[:, :part]], axis=1),
            jnp.concatenate([pack[:, wide : 2 * wide], rest[:, part : 2 * part]], axis=1),
        )
        share[...] = jnp.broadcast_to(share_of(plain, expand[0]), (8, LANES))
        scale = column_of(rounded(gain[...]))
        for c, grad in enumerate(plain):
            adam_store(c, grad * scale, RATE_MATRIX, *expand)
        grad = jnp.concatenate([pack[:, 5 * LANES :], rest[:, 2 * part : 3 * part]], axis=1)
        adam_store(Ellipsis, grad.T, RATE_MATRIX, *reduce)

    return body


def gain_step_kernel(*refs):
    parts, refs = refs[:4], refs[4:]
    total = parts[0][...] + parts[1][...] + parts[2][...] + parts[3][...]
    count = refs[0].shape[1]
    for i in range(2):
        adam_store(Ellipsis, total[i : i + 1, :count], RATE_GAIN, *refs[i::2])


def pack_attend(gain, triple, merge):
    folded = (gain.astype(BF16).astype(F32)[:, None] * triple.astype(BF16).astype(F32)).astype(BF16)
    turned = merge.astype(BF16).T
    q, k, v = folded[0], folded[1], folded[2]
    return jnp.concatenate(
        [
            q[:, :LANES],
            k[:, :LANES],
            q[:, LANES:],
            k[:, LANES:],
            v[:, :LANES],
            v[:, LANES:],
            turned[:, LANES:],
            turned[:, :LANES],
        ],
        axis=1,
    )


def unpack_attend(pack, gain):
    scale = gain.astype(BF16).astype(F32)[:, None]
    q = jnp.concatenate([pack[:, :LANES], pack[:, 2 * LANES : 2 * LANES + HD]], axis=1)
    k = jnp.concatenate([pack[:, LANES : 2 * LANES], pack[:, 2 * LANES + HD : 3 * LANES]], axis=1)
    v = jnp.concatenate([pack[:, 3 * LANES : 4 * LANES], pack[:, 4 * LANES : 4 * LANES + HD]], axis=1)
    plain = jnp.stack([q, k, v])
    merge = jnp.concatenate([pack[:, 5 * LANES :], pack[:, 4 * LANES + HD : 5 * LANES]], axis=1).T
    return plain, plain * scale, merge


def pack_feed(gain, expand, reduce):
    folded = (gain.astype(BF16).astype(F32)[:, None] * expand.astype(BF16).astype(F32)).astype(BF16)
    turned = reduce.astype(BF16).T
    wide = 2 * LANES
    spare = jnp.zeros((turned.shape[0], LANES // 4), BF16)
    return jnp.concatenate(
        [
            folded[0][:, :wide],
            folded[1][:, :wide],
            folded[0][:, wide:],
            folded[1][:, wide:],
            turned[:, wide:],
            spare,
            turned[:, :wide],
        ],
        axis=1,
    )


def unpack_feed(pack, gain):
    scale = gain.astype(BF16).astype(F32)[:, None]
    wide, part = 2 * LANES, LANES // 4
    rest = pack[:, 4 * LANES : 5 * LANES]
    one = jnp.concatenate([pack[:, :wide], rest[:, :part]], axis=1)
    two = jnp.concatenate([pack[:, wide : 2 * wide], rest[:, part : 2 * part]], axis=1)
    plain = jnp.stack([one, two])
    reduce = jnp.concatenate([pack[:, 5 * LANES :], rest[:, 2 * part : 3 * part]], axis=1).T
    return plain, plain * scale, reduce


def make_on_device(sizes):
    dp, mp = sizes["dp"], sizes["mp"]
    direct = dp == 8

    def over_mp(value, step):
        return lax.ppermute(value, "mp", [(i, i ^ step) for i in range(mp)])

    def over_dp(value, step):
        return lax.ppermute(value, "dp", [(i, i ^ step) for i in range(dp)])

    def gather_chunks(shard):
        if not direct:
            return [lax.all_gather(shard, "dp", axis=0, tiled=True)]
        along = [shard] + [over_dp(shard, s) for s in (2, 4, 6)]
        across = [over_dp(piece, 1) for piece in along]
        return [piece for pair in zip(along, across) for piece in pair]

    def reduce_chunks(chunks):
        if not direct:
            return [lax.psum_scatter(chunks[0], "dp", scatter_dimension=0, tiled=True)]
        groups = len(chunks) // 2
        found = []
        for g in range(groups):
            mine, send = chunks[2 * g], chunks[2 * g + 1]
            got = over_dp(send, 1)
            first = g * mine.shape[0]
            outs = [
                (mine.shape[1:], BF16 if first + i else F32) for i in range(mine.shape[0])
            ]
            sums = run_kernel(chunk_sum_kernel, outs, (mine, got))
            for i, part in enumerate(sums):
                step = 2 * (first + i)
                found.append(over_dp(part, step) if step else part)
        return found

    def reduce_pairs(pairs):
        if not direct:
            return [lax.psum_scatter(pairs[0], "dp", scatter_dimension=0, tiled=True)]
        got = [over_dp(pairs[i], 2 * i) for i in range(1, dp // 2 - 1)]
        mine, send = pairs[-2:]
        shape = mine.shape
        (last,) = run_kernel(near_sum_kernel, [(shape, BF16)], (mine, over_dp(send, 1)))
        last = over_dp(last, dp - 2)
        mine, send = run_kernel(pair_sum_kernel, [(shape, F32), (shape, BF16)], (pairs[0], *got))
        return [mine, over_dp(send, 1), last]

    def on_device(
        block_input,
        out_cotangent,
        gain_attend,
        weight_triple,
        weight_merge,
        gain_feed,
        weight_expand,
        weight_reduce,
        *moments,
    ):
        rows, width = block_input.shape
        length = rows * mp
        chunks = dp if direct else 1
        deep = width // chunks
        me, here = lax.axis_index("mp"), lax.axis_index("dp")
        places = jnp.bitwise_xor(me, jnp.arange(4, dtype=jnp.int32)) * rows
        if direct:
            spots = jnp.bitwise_xor(here, jnp.arange(dp, dtype=jnp.int32)) * deep
        else:
            spots = jnp.zeros((1,), jnp.int32)
        cosine, sine = (jnp.asarray(table) for table in rope_tables(length))

        def spread_rows(value):
            far = over_mp(value, 2)
            near = over_mp(value, 1)
            return [value, near, far, over_mp(far, 1)]

        if direct:
            gain_row, feed_row = gain_attend.reshape(1, deep), gain_feed.reshape(1, deep)
            (first_pack,) = run_kernel(
                pack_attend_kernel,
                [((deep, 6 * LANES), BF16)],
                (gain_row, weight_triple, weight_merge),
            )
            (second_pack,) = run_kernel(
                pack_feed_kernel,
                [((deep, 7 * LANES), BF16)],
                (feed_row, weight_expand, weight_reduce),
            )
        else:
            first_pack = pack_attend(gain_attend, weight_triple, weight_merge)
            second_pack = pack_feed(gain_feed, weight_expand, weight_reduce)
        (own,) = run_kernel(
            prepare_kernel,
            [((rows, 2 * width), BF16)],
            (places, spots, block_input, out_cotangent),
            scalars=2,
        )
        first_chunks = gather_chunks(first_pack)
        blocks = spread_rows(own)
        second_chunks = gather_chunks(second_pack)

        half_rows = (2, rows, width)
        pad = length + WINDOW
        normed, cot, weight, qkv, att, lse, keep, send = run_kernel(
            make_attend(length, width, rows, chunks),
            [
                ((length, width), BF16),
                ((length, width), BF16),
                ((width, 6 * LANES), BF16),
                ((length, 5 * LANES), BF16),
                ((length, 2 * LANES), BF16),
                ((length, LANES), F32),
                (half_rows, F32),
                (half_rows, BF16),
            ],
            (places, spots, cosine, sine, *blocks, *first_chunks),
            scalars=2,
            scratch=[pltpu.VMEM((pad, LANES), BF16)] * 4 + [pltpu.VMEM((length, width), F32)],
        )

        def to_owner(keep, send):
            mine, far = run_kernel(
                core_sum_kernel,
                [((rows, width), F32), ((rows, width), BF16)],
                (keep, over_mp(send, 1)),
            )
            return mine, over_mp(far, 2)

        mine, got = to_owner(keep, send)
        residual, normed_two = run_kernel(
            second_norm_kernel,
            [((rows, width), F32), ((rows, width), BF16)],
            (block_input, mine, got),
        )
        blocks = spread_rows(normed_two)
        normed_two_all, d_all, inner_all, keep_s, send_s, keep_o, send_o = run_kernel(
            make_feed(length, width, rows, chunks),
            [
                ((length, width), BF16),
                ((length, 5 * LANES), BF16),
                ((length, 3 * LANES), BF16),
                (half_rows, F32),
                (half_rows, BF16),
                (half_rows, F32),
                (half_rows, BF16),
            ],
            (places, spots, *blocks, cot, *second_chunks),
            scalars=2,
            scratch=[pltpu.VMEM((width, 7 * LANES), BF16), pltpu.VMEM((length, width), F32)],
        )
        mine, got = to_owner(keep_s, send_s)
        out_mine, out_got = to_owner(keep_o, send_o)
        feed_chunks = run_kernel(
            make_feed_grads(chunks),
            pair_outs(chunks, deep, 7 * LANES),
            (spots, normed_two_all, cot, d_all, inner_all),
            scalars=1,
            scratch=[pltpu.VMEM((width, 7 * LANES), F32)],
        )
        d_residual, residual_b = run_kernel(
            residual_back_kernel,
            [((rows, width), F32), ((rows, width), BF16)],
            (out_cotangent, residual, mine, got),
        )
        blocks = spread_rows(residual_b)
        feed_parts = reduce_pairs(feed_chunks)
        d_pre, *attend_chunks = run_kernel(
            make_attend_back(length, width, rows, chunks),
            [((length, 5 * LANES), BF16)] + chunk_outs(chunks, deep, 6 * LANES, 2),
            (places, spots, cosine, sine, *blocks, normed, weight, qkv, att, lse),
            scalars=2,
            scratch=[
                pltpu.VMEM((length, width), BF16),
                pltpu.VMEM((width, 6 * LANES), F32),
            ]
            + [pltpu.VMEM((pad, LANES), BF16)] * 4
            + [pltpu.VMEM((length, 2 * LANES), BF16)]
            + [pltpu.VMEM((pad, LANES), F32)] * 4,
        )
        attend_parts = reduce_chunks(attend_chunks)
        keep, send = run_kernel(
            make_input_share(rows),
            [(half_rows, F32), (half_rows, BF16)],
            (places, d_pre, weight),
            scalars=1,
            scratch=[pltpu.VMEM((length, width), F32)],
        )
        mine, got = to_owner(keep, send)
        input_grad, block_output = run_kernel(
            finish_kernel,
            [((rows, width), F32), ((rows, width), F32)],
            (block_input, d_residual, mine, got, residual, out_mine, out_got),
            final=True,
        )

        if direct:
            shapes = [item.shape for item in (weight_expand, weight_reduce)]
            *feed_new, share = run_kernel(
                make_adam_feed(len(feed_parts)),
                [(shape, F32) for shape in shapes * 4] + [((8, LANES), F32)],
                (*feed_parts, feed_row, weight_expand, weight_reduce)
                + (moments[4], moments[5], moments[10], moments[11]),
                final=True,
            )

            (share,) = run_kernel(
                make_share(len(attend_parts)),
                [((8, LANES), F32)],
                (*attend_parts, weight_triple, share),
            )
            got = [over_mp(share, step) for step in (2, 3, 1)]
            gain_new = run_kernel(
                gain_step_kernel,
                [((1, deep), F32)] * 8,
                (share, *got, gain_row, feed_row)
                + tuple(moments[i].reshape(1, deep) for i in (0, 3, 6, 9)),
                final=True,
            )
            shapes = [item.shape for item in (weight_triple, weight_merge)]
            attend_new = run_kernel(
                make_adam_attend(len(attend_parts)),
                [(shape, F32) for shape in shapes * 4],
                (*attend_parts, gain_row, weight_triple, weight_merge)
                + (moments[1], moments[2], moments[7], moments[8]),
                final=True,
            )
            gain_new = [item.reshape(deep) for item in gain_new]
            grads, fresh, first_new, second_new = (
                (gain_new[i], attend_new[i], attend_new[i + 1])
                + (gain_new[i + 1], feed_new[i], feed_new[i + 1])
                for i in (0, 2, 4, 6)
            )
        else:
            plain_triple, grad_triple, grad_merge = unpack_attend(attend_parts[0], gain_attend)
            plain_expand, grad_expand, grad_reduce = unpack_feed(feed_parts[0], gain_feed)
            grads = (
                lax.psum(jnp.sum(plain_triple * rounded(weight_triple), axis=(0, 2)), "mp"),
                grad_triple,
                grad_merge,
                lax.psum(jnp.sum(plain_expand * rounded(weight_expand), axis=(0, 2)), "mp"),
                grad_expand,
                grad_reduce,
            )
            weights = (gain_attend, weight_triple, weight_merge)
            weights += (gain_feed, weight_expand, weight_reduce)
            rates = (RATE_GAIN, RATE_MATRIX, RATE_MATRIX) * 2
            stepped = [
                adam_step(weight, first, second, grad, rate)
                for weight, first, second, grad, rate in zip(
                    weights, moments[:6], moments[6:], grads, rates
                )
            ]
            fresh, first_new, second_new = (tuple(item[i] for item in stepped) for i in range(3))
        return (block_output, input_grad) + grads + fresh + first_new + second_new

    return on_device


def solution(mesh):
    rows = P(("dp", "mp"), None)
    params = (P("dp"), P(None, "dp", "mp"), P("mp", "dp"), P("dp"), P(None, "dp", "mp"), P("mp", "dp"))
    sizes = dict(mesh.shape)
    inner = make_on_device(sizes)

    return jax.shard_map(
        inner,
        mesh=mesh,
        in_specs=(rows, rows) + params * 3,
        out_specs=(rows, rows) + params * 4,
        check_vma=False,
    )
```

profile of v0, /device:TPU:0, one launch (start us, length us, event | category | flops | bytes accessed | tf_op | source)
XLA Modules:
  0.0 148.9 jit_solution(719458938484177007)
XLA Ops:
  3.5 3.0 %collective-permute-start.1 = (bf16[128,1536]{1,0:T(8,128)(2,1)S(1)}, bf16[128,1536]{1,0:T(8,128)(2,1)S(1)}, u32[]{:S(2)}, u32[]{:S(2)}) collective-permute-start(bf16[128,1536]{1,0:T(8,128)(2,1)S(1)} %shard_map.413.refs_0_), channel_id=1, source_target_pairs={{0,2},{1,3},{2,0},{3,1},{4,6},{5,7},{6,4},{7,5},{8,10},{9,11},{10,... | collective-permute-start | bytes 1179656 | tf_op jit(solution)/shard_map/ppermute | solution.py:666
  6.7 3.7 %collective-permute-start.8 = (bf16[96,768]{1,0:T(8,128)(2,1)S(1)}, bf16[96,768]{1,0:T(8,128)(2,1)S(1)}, u32[]{:S(2)}, u32[]{:S(2)}) collective-permute-start(bf16[96,768]{1,0:T(8,128)(2,1)S(1)} %shard_map.414.refs_4_), channel_id=1, source_target_pairs={{0,24},{4,28},{8,16},{12,20},{16,8},{20,12},{24,0},{28,4},{1,25},{... | collective-permute-start | bytes 442376 | tf_op jit(solution)/shard_map/ppermute | solution.py:669
  10.4 5.2 %collective-permute-done.1.refs_2_ = bf16[128,1536]{1,0:T(8,128)(2,1)S(1)} collective-permute-done((bf16[128,1536]{1,0:T(8,128)(2,1)S(1)}, bf16[128,1536]{1,0:T(8,128)(2,1)S(1)}, u32[]{:S(2)}, u32[]{:S(2)}) %collective-permute-start.1) | collective-permute-done | bytes 393248 | tf_op jit(solution)/shard_map/ppermute | solution.py:666
  15.6 2.8 %collective-permute-start.6 = (bf16[96,768]{1,0:T(8,128)(2,1)S(1)}, bf16[96,768]{1,0:T(8,128)(2,1)S(1)}, u32[]{:S(2)}, u32[]{:S(2)}) collective-permute-start(bf16[96,768]{1,0:T(8,128)(2,1)S(1)} %shard_map.414.refs_4_), channel_id=1, source_target_pairs={{0,16},{4,20},{8,24},{12,28},{16,0},{20,4},{24,8},{28,12},{1,17},{... | collective-permute-start | bytes 442376 | tf_op jit(solution)/shard_map/ppermute | solution.py:669
  18.5 1.6 %collective-permute-start.4 = (bf16[96,768]{1,0:T(8,128)(2,1)S(1)}, bf16[96,768]{1,0:T(8,128)(2,1)S(1)}, u32[]{:S(2)}, u32[]{:S(2)}) collective-permute-start(bf16[96,768]{1,0:T(8,128)(2,1)S(1)} %shard_map.414.refs_4_), channel_id=1, source_target_pairs={{0,8},{4,12},{8,0},{12,4},{16,24},{20,28},{24,16},{28,20},{1,9},{5... | collective-permute-start | bytes 442376 | tf_op jit(solution)/shard_map/ppermute | solution.py:669
  21.6 4.7 %collective-permute-done.6.refs_8_ = bf16[96,768]{1,0:T(8,128)(2,1)S(1)} collective-permute-done((bf16[96,768]{1,0:T(8,128)(2,1)S(1)}, bf16[96,768]{1,0:T(8,128)(2,1)S(1)}, u32[]{:S(2)}, u32[]{:S(2)}) %collective-permute-start.6) | collective-permute-done | bytes 147488 | tf_op jit(solution)/shard_map/ppermute | solution.py:669
  29.9 3.1 %collective-permute-done.9.refs_11_ = bf16[96,768]{1,0:T(8,128)(2,1)S(1)} collective-permute-done((bf16[96,768]{1,0:T(8,128)(2,1)S(1)}, bf16[96,768]{1,0:T(8,128)(2,1)S(1)}, u32[]{:S(2)}, u32[]{:S(2)}) %collective-permute-start.9) | collective-permute-done | bytes 147488 | tf_op jit(solution)/shard_map/ppermute | solution.py:669
  33.0 3.2 %collective-permute-done.7.refs_9_ = bf16[96,768]{1,0:T(8,128)(2,1)S(1)} collective-permute-done((bf16[96,768]{1,0:T(8,128)(2,1)S(1)}, bf16[96,768]{1,0:T(8,128)(2,1)S(1)}, u32[]{:S(2)}, u32[]{:S(2)}) %collective-permute-start.7) | collective-permute-done | bytes 147488 | tf_op jit(solution)/shard_map/ppermute | solution.py:669
  36.1 2.0 %collective-permute-done.5.refs_7_ = bf16[96,768]{1,0:T(8,128)(2,1)S(1)} collective-permute-done((bf16[96,768]{1,0:T(8,128)(2,1)S(1)}, bf16[96,768]{1,0:T(8,128)(2,1)S(1)}, u32[]{:S(2)}, u32[]{:S(2)}) %collective-permute-start.5) | collective-permute-done | bytes 147488 | tf_op jit(solution)/shard_map/ppermute | solution.py:669
  38.1 4.5 %shard_map.415 = (bf16[512,768]{1,0:T(8,128)(2,1)S(1)}, bf16[512,768]{1,0:T(8,128)(2,1)S(1)}, bf16[768,768]{1,0:T(8,128)(2,1)S(1)}, bf16[512,640]{1,0:T(8,128)(2...) custom-call(s32[4]{0:T(128)S(1)} %xor_multiply_fusion.1.places, ...), custom_call_target="tpu_custom_call" | custom-call | tf_op jit(solution)/shard_map/pallas_call | solution.py:44
  42.8 1.7 %collective-permute-done.10.got_ref = bf16[2,128,768]{2,1,0:T(8,128)(2,1)S(1)} collective-permute-done((bf16[2,128,768]{2,1,0:T(8,128)(2,1)S(1)}, bf16[2,128,768]{2,1,0:T(8,128)(2,1)S(1)}, u32[]{:S(2)}, u32[]{:S(2)}) %collective-permute-start.10) | collective-permute-done | bytes 393248 | tf_op jit(solution)/shard_map/ppermute | solution.py:666
  46.0 5.6 %collective-permute-done.11.got_ref = bf16[128,768]{1,0:T(8,128)(2,1)S(1)} collective-permute-done((bf16[128,768]{1,0:T(8,128)(2,1)S(1)}, bf16[128,768]{1,0:T(8,128)(2,1)S(1)}, u32[]{:S(2)}, u32[]{:S(2)}) %collective-permute-start.11) | collective-permute-done | bytes 196640 | tf_op jit(solution)/shard_map/ppermute | solution.py:666
  53.5 3.9 %collective-permute-start.20 = (bf16[96,896]{1,0:T(8,128)(2,1)S(1)}, bf16[96,896]{1,0:T(8,128)(2,1)S(1)}, u32[]{:S(2)}, u32[]{:S(2)}) collective-permute-start(bf16[96,896]{1,0:T(8,128)(2,1)S(1)} %shard_map.418.refs_5_), channel_id=1, source_target_pairs={{0,24},{4,28},{8,16},{12,20},{16,8},{20,12},{24,0},{28,4},{1,25},{... | collective-permute-start | bytes 516104 | tf_op jit(solution)/shard_map/ppermute | solution.py:669
  59.6 3.1 %collective-permute-done.20.refs_11_ = bf16[96,896]{1,0:T(8,128)(2,1)S(1)} collective-permute-done((bf16[96,896]{1,0:T(8,128)(2,1)S(1)}, bf16[96,896]{1,0:T(8,128)(2,1)S(1)}, u32[]{:S(2)}, u32[]{:S(2)}) %collective-permute-start.20) | collective-permute-done | bytes 172064 | tf_op jit(solution)/shard_map/ppermute | solution.py:669
  63.2 7.2 %collective-permute-done.18.refs_9_ = bf16[96,896]{1,0:T(8,128)(2,1)S(1)} collective-permute-done((bf16[96,896]{1,0:T(8,128)(2,1)S(1)}, bf16[96,896]{1,0:T(8,128)(2,1)S(1)}, u32[]{:S(2)}, u32[]{:S(2)}) %collective-permute-start.18) | collective-permute-done | bytes 172064 | tf_op jit(solution)/shard_map/ppermute | solution.py:669
  73.9 3.7 %collective-permute-done.21.refs_12_ = bf16[96,896]{1,0:T(8,128)(2,1)S(1)} collective-permute-done((bf16[96,896]{1,0:T(8,128)(2,1)S(1)}, bf16[96,896]{1,0:T(8,128)(2,1)S(1)}, u32[]{:S(2)}, u32[]{:S(2)}) %collective-permute-start.21) | collective-permute-done | bytes 172064 | tf_op jit(solution)/shard_map/ppermute | solution.py:669
  77.6 2.9 %collective-permute-done.19.refs_10_ = bf16[96,896]{1,0:T(8,128)(2,1)S(1)} collective-permute-done((bf16[96,896]{1,0:T(8,128)(2,1)S(1)}, bf16[96,896]{1,0:T(8,128)(2,1)S(1)}, u32[]{:S(2)}, u32[]{:S(2)}) %collective-permute-start.19) | collective-permute-done | bytes 172064 | tf_op jit(solution)/shard_map/ppermute | solution.py:669
  80.5 1.8 %collective-permute-done.17.refs_8_ = bf16[96,896]{1,0:T(8,128)(2,1)S(1)} collective-permute-done((bf16[96,896]{1,0:T(8,128)(2,1)S(1)}, bf16[96,896]{1,0:T(8,128)(2,1)S(1)}, u32[]{:S(2)}, u32[]{:S(2)}) %collective-permute-start.17) | collective-permute-done | bytes 172064 | tf_op jit(solution)/shard_map/ppermute | solution.py:669
  82.4 3.4 %shard_map.419 = (bf16[512,768]{1,0:T(8,128)(2,1)S(1)}, bf16[512,640]{1,0:T(8,128)(2,1)S(1)}, bf16[512,384]{1,0:T(8,128)(2,1)S(1)}, f32[2,128,768]{2,1,0:T(8,128...) custom-call(s32[4]{0:T(128)S(1)} %xor_multiply_fusion.1.places, ...), custom_call_target="tpu_custom_call" | custom-call | tf_op jit(solution)/shard_map/pallas_call | solution.py:44
  85.9 1.7 %collective-permute-done.22.got_ref = bf16[2,128,768]{2,1,0:T(8,128)(2,1)S(1)} collective-permute-done((bf16[2,128,768]{2,1,0:T(8,128)(2,1)S(1)}, bf16[2,128,768]{2,1,0:T(8,128)(2,1)S(1)}, u32[]{:S(2)}, u32[]{:S(2)}) %collective-permute-start.22) | collective-permute-done | bytes 393248 | tf_op jit(solution)/shard_map/ppermute | solution.py:666
  88.3 6.4 %collective-permute-done.23.got_ref = bf16[128,768]{1,0:T(8,128)(2,1)S(1)} collective-permute-done((bf16[128,768]{1,0:T(8,128)(2,1)S(1)}, bf16[128,768]{1,0:T(8,128)(2,1)S(1)}, u32[]{:S(2)}, u32[]{:S(2)}) %collective-permute-start.23) | collective-permute-done | bytes 196640 | tf_op jit(solution)/shard_map/ppermute | solution.py:666
  95.6 1.9 %shard_map.429 = (f32[2,96,896]{2,1,0:T(8,128)S(1)}, bf16[2,96,896]{2,1,0:T(8,128)(2,1)S(1)}, bf16[2,96,896]{2,1,0:T(8,128)(2,1)S(1)}, f32[96,896]{1,0:T(8,128)S(1)}, bf16[96,896]{1,0:T(8,128)(2,1)S(1)}) custom-call(s32[8]{0:T(128)S(1)} %xor_multiply_fusion.spots, bf16[512,768]{1,0:T(8,128)(2,1)S(1)} %get-tuple-element.135.normed, ...), custom_call_target="tpu_custom_call" | custom-call | tf_op jit(solution)/shard_map/pallas_call | solution.py:44
  98.5 2.7 %collective-permute-done.25.refs_2_ = bf16[128,768]{1,0:T(8,128)(2,1)S(1)} collective-permute-done((bf16[128,768]{1,0:T(8,128)(2,1)S(1)}, bf16[128,768]{1,0:T(8,128)(2,1)S(1)}, u32[]{:S(2)}, u32[]{:S(2)}) %collective-permute-start.25) | collective-permute-done | bytes 196640 | tf_op jit(solution)/shard_map/ppermute | solution.py:666
  103.2 5.7 %shard_map.422 = (bf16[512,640]{1,0:T(8,128)(2,1)S(1)}, f32[2,96,768]{2,1,0:T(8,128)S(1)}, bf16[2,96,768]{2,1,0:T(8,128)(2,1)S(1)}, f32[2,96,768]{2,1,0:T(8,128)S(1)}, bf16[2,96,768]{2,1,0:T(8,128)(2,1)S(1)}) custom-call(s32[4]{0:T(128)S(1)} %xor_multiply_fusion.1.places, s32[8]{0:T(128)S(1)} %xor_multiply_fusion.spots, f32[512,128]{1,0:T(8,128)S(1)} %copy-done.7, ...), custom_call_target="tpu_custom_call" | custom-call | tf_op jit(solution)/shard_map/pallas_call | solution.py:44
  113.3 6.7 %collective-permute-done.37.refs_2_ = bf16[2,96,896]{2,1,0:T(8,128)(2,1)S(1)} collective-permute-done((bf16[2,96,896]{2,1,0:T(8,128)(2,1)S(1)}, bf16[2,96,896]{2,1,0:T(8,128)(2,1)S(1)}, u32[]{:S(2)}, u32[]{:S(2)}) %collective-permute-start.37) | collective-permute-done | bytes 344096 | tf_op jit(solution)/shard_map/ppermute | solution.py:669
  120.0 2.7 %collective-permute-start.40 = (bf16[96,896]{1,0:T(8,128)(2,1)S(1)}, bf16[96,896]{1,0:T(8,128)(2,1)S(1)}, u32[]{:S(2)}, u32[]{:S(2)}) collective-permute-start(bf16[96,896]{1,0:T(8,128)(2,1)S(1)} %shard_map.431), channel_id=1, source_target_pairs={{0,24},{4,28},{8,16},{12,20},{16,8},{20,12},{24,0},{28,4},{1,25},{... | collective-permute-start | bytes 516104 | tf_op jit(solution)/shard_map/ppermute | solution.py:669
  122.8 1.6 %collective-permute-start.38 = (bf16[96,896]{1,0:T(8,128)(2,1)S(1)}, bf16[96,896]{1,0:T(8,128)(2,1)S(1)}, u32[]{:S(2)}, u32[]{:S(2)}) collective-permute-start(bf16[96,896]{1,0:T(8,128)(2,1)S(1)} %get-tuple-element.142), channel_id=1, source_target_pairs={{0,4},{4,0},{8,12},{12,8},{16,20},{20,16},{24,28},{28,24},{1,5},{5... | collective-permute-start | bytes 516104 | tf_op jit(solution)/shard_map/ppermute | solution.py:669
  125.2 1.6 %collective-permute-start.28 = (bf16[128,768]{1,0:T(8,128)(2,1)S(1)}, bf16[128,768]{1,0:T(8,128)(2,1)S(1)}, u32[]{:S(2)}, u32[]{:S(2)}) collective-permute-start(bf16[128,768]{1,0:T(8,128)(2,1)S(1)} %get-tuple-element.120), channel_id=1, source_target_pairs={{0,2},{1,3},{2,0},{3,1},{4,6},{5,7},{6,4},{7,5},{8,10},{9,11},{10,... | collective-permute-start | bytes 589832 | tf_op jit(solution)/shard_map/ppermute | solution.py:666
  126.8 2.9 %collective-permute-start.32 = (bf16[96,768]{1,0:T(8,128)(2,1)S(1)}, bf16[96,768]{1,0:T(8,128)(2,1)S(1)}, u32[]{:S(2)}, u32[]{:S(2)}) collective-permute-start(bf16[96,768]{1,0:T(8,128)(2,1)S(1)} %get-tuple-element.130), channel_id=1, source_target_pairs={{0,8},{4,12},{8,0},{12,4},{16,24},{20,28},{24,16},{28,20},{1,9},{5... | collective-permute-start | bytes 442376 | tf_op jit(solution)/shard_map/ppermute | solution.py:669
  130.6 2.4 %collective-permute-start.35 = (bf16[96,768]{1,0:T(8,128)(2,1)S(1)}, bf16[96,768]{1,0:T(8,128)(2,1)S(1)}, u32[]{:S(2)}, u32[]{:S(2)}) collective-permute-start(bf16[96,768]{1,0:T(8,128)(2,1)S(1)} %get-tuple-element.134), channel_id=1, source_target_pairs={{0,24},{4,28},{8,16},{12,20},{16,8},{20,12},{24,0},{28,4},{1,25},{... | collective-permute-start | bytes 442376 | tf_op jit(solution)/shard_map/ppermute | solution.py:669
  133.1 1.7 %shard_map.432 = (f32[2,96,288]{2,1,0:T(8,128)}, f32[288,96]{1,0:T(8,128)}, f32[2,96,288]{2,1,0:T(8,128)}, f32[288,96]{1,0:T(8,128)}, f32[2,96,288]{2,1,0:T(8,12...) custom-call(f32[96,896]{1,0:T(8,128)S(1)} %get-tuple-element.141.refs_0_, ...), custom_call_target="tpu_custom_call" | custom-call | tf_op jit(solution)/shard_map/pallas_call | solution.py:44
  134.8 7.8 %collective-permute-done.34.refs_2_ = bf16[96,768]{1,0:T(8,128)(2,1)S(1)} collective-permute-done((bf16[96,768]{1,0:T(8,128)(2,1)S(1)}, bf16[96,768]{1,0:T(8,128)(2,1)S(1)}, u32[]{:S(2)}, u32[]{:S(2)}) %collective-permute-start.34) | collective-permute-done | bytes 147488 | tf_op jit(solution)/shard_map/ppermute | solution.py:669
  (129 shorter events, 34.9 us)
Async XLA Ops:
  3.5 12.1 %collective-permute-start.1 = (bf16[128,1536]{1,0:T(8,128)(2,1)S(1)}, bf16[128,1536]{1,0:T(8,128)(2,1)S(1)}, u32[]{:S(2)}, u32[]{:S(2)}) collective-permute-start(bf16[128,1536]{1,0:T(8,128)(2,1)S(1)} %shard_map.413.refs_0_), channel_id=1, source_target_pairs={{0,2},{1,3},{2,0},{3,1},{4,6},{5,7},{6,4},{7,5},{8,10},{9,11},{10,... | collective-permute-start | bytes 1179656 | tf_op jit(solution)/shard_map/ppermute | solution.py:666
  6.7 13.3 %collective-permute-start.8 = (bf16[96,768]{1,0:T(8,128)(2,1)S(1)}, bf16[96,768]{1,0:T(8,128)(2,1)S(1)}, u32[]{:S(2)}, u32[]{:S(2)}) collective-permute-start(bf16[96,768]{1,0:T(8,128)(2,1)S(1)} %shard_map.414.refs_4_), channel_id=1, source_target_pairs={{0,24},{4,28},{8,16},{12,20},{16,8},{20,12},{24,0},{28,4},{1,25},{... | collective-permute-start | bytes 442376 | tf_op jit(solution)/shard_map/ppermute | solution.py:669
  10.4 27.7 %collective-permute-start = (bf16[128,1536]{1,0:T(8,128)(2,1)S(1)}, bf16[128,1536]{1,0:T(8,128)(2,1)S(1)}, u32[]{:S(2)}, u32[]{:S(2)}) collective-permute-start(bf16[128,1536]{1,0:T(8,128)(2,1)S(1)} %shard_map.413.refs_0_), channel_id=1, source_target_pairs={{0,1},{1,0},{2,3},{3,2},{4,5},{5,4},{6,7},{7,6},{8,9},{9,8},{10,11... | collective-permute-start | bytes 1179656 | tf_op jit(solution)/shard_map/ppermute | solution.py:666
  15.6 22.5 %collective-permute-start.2 = (bf16[128,1536]{1,0:T(8,128)(2,1)S(1)}, bf16[128,1536]{1,0:T(8,128)(2,1)S(1)}, u32[]{:S(2)}, u32[]{:S(2)}) collective-permute-start(bf16[128,1536]{1,0:T(8,128)(2,1)S(1)} %collective-permute-done.1.refs_2_), channel_id=1, source_target_pairs={{0,1},{1,0},{2,3},{3,2},{4,5},{5,4},{6,7},{7,6},{8,9},{9,8},{10,11... | collective-permute-start | bytes 1179656 | tf_op jit(solution)/shard_map/ppermute | solution.py:666
  15.6 10.6 %collective-permute-start.6 = (bf16[96,768]{1,0:T(8,128)(2,1)S(1)}, bf16[96,768]{1,0:T(8,128)(2,1)S(1)}, u32[]{:S(2)}, u32[]{:S(2)}) collective-permute-start(bf16[96,768]{1,0:T(8,128)(2,1)S(1)} %shard_map.414.refs_4_), channel_id=1, source_target_pairs={{0,16},{4,20},{8,24},{12,28},{16,0},{20,4},{24,8},{28,12},{1,17},{... | collective-permute-start | bytes 442376 | tf_op jit(solution)/shard_map/ppermute | solution.py:669
  18.5 9.4 %collective-permute-start.4 = (bf16[96,768]{1,0:T(8,128)(2,1)S(1)}, bf16[96,768]{1,0:T(8,128)(2,1)S(1)}, u32[]{:S(2)}, u32[]{:S(2)}) collective-permute-start(bf16[96,768]{1,0:T(8,128)(2,1)S(1)} %shard_map.414.refs_4_), channel_id=1, source_target_pairs={{0,8},{4,12},{8,0},{12,4},{16,24},{20,28},{24,16},{28,20},{1,9},{5... | collective-permute-start | bytes 442376 | tf_op jit(solution)/shard_map/ppermute | solution.py:669
  20.1 8.2 %collective-permute-start.3 = (bf16[96,768]{1,0:T(8,128)(2,1)S(1)}, bf16[96,768]{1,0:T(8,128)(2,1)S(1)}, u32[]{:S(2)}, u32[]{:S(2)}) collective-permute-start(bf16[96,768]{1,0:T(8,128)(2,1)S(1)} %shard_map.414.refs_4_), channel_id=1, source_target_pairs={{0,4},{4,0},{8,12},{12,8},{16,20},{20,16},{24,28},{28,24},{1,5},{5... | collective-permute-start | bytes 442376 | tf_op jit(solution)/shard_map/ppermute | solution.py:669
  27.8 8.3 %collective-permute-start.7 = (bf16[96,768]{1,0:T(8,128)(2,1)S(1)}, bf16[96,768]{1,0:T(8,128)(2,1)S(1)}, u32[]{:S(2)}, u32[]{:S(2)}) collective-permute-start(bf16[96,768]{1,0:T(8,128)(2,1)S(1)} %collective-permute-done.6.refs_8_), channel_id=1, source_target_pairs={{0,4},{4,0},{8,12},{12,8},{16,20},{20,16},{24,28},{28,24},{1,5},{5... | collective-permute-start | bytes 442376 | tf_op jit(solution)/shard_map/ppermute | solution.py:669
  28.3 9.8 %collective-permute-start.5 = (bf16[96,768]{1,0:T(8,128)(2,1)S(1)}, bf16[96,768]{1,0:T(8,128)(2,1)S(1)}, u32[]{:S(2)}, u32[]{:S(2)}) collective-permute-start(bf16[96,768]{1,0:T(8,128)(2,1)S(1)} %collective-permute-done.4.refs_6_), channel_id=1, source_target_pairs={{0,4},{4,0},{8,12},{12,8},{16,20},{20,16},{24,28},{28,24},{1,5},{5... | collective-permute-start | bytes 442376 | tf_op jit(solution)/shard_map/ppermute | solution.py:669
  51.8 10.8 %collective-permute-start.13 = (bf16[128,768]{1,0:T(8,128)(2,1)S(1)}, bf16[128,768]{1,0:T(8,128)(2,1)S(1)}, u32[]{:S(2)}, u32[]{:S(2)}) collective-permute-start(bf16[128,768]{1,0:T(8,128)(2,1)S(1)} %get-tuple-element.103.refs_0_), channel_id=1, source_target_pairs={{0,2},{1,3},{2,0},{3,1},{4,6},{5,7},{6,4},{7,5},{8,10},{9,11},{10,... | collective-permute-start | bytes 589832 | tf_op jit(solution)/shard_map/ppermute | solution.py:666
  53.5 9.2 %collective-permute-start.20 = (bf16[96,896]{1,0:T(8,128)(2,1)S(1)}, bf16[96,896]{1,0:T(8,128)(2,1)S(1)}, u32[]{:S(2)}, u32[]{:S(2)}) collective-permute-start(bf16[96,896]{1,0:T(8,128)(2,1)S(1)} %shard_map.418.refs_5_), channel_id=1, source_target_pairs={{0,24},{4,28},{8,16},{12,20},{16,8},{20,12},{24,0},{28,4},{1,25},{... | collective-permute-start | bytes 516104 | tf_op jit(solution)/shard_map/ppermute | solution.py:669
  57.4 13.0 %collective-permute-start.18 = (bf16[96,896]{1,0:T(8,128)(2,1)S(1)}, bf16[96,896]{1,0:T(8,128)(2,1)S(1)}, u32[]{:S(2)}, u32[]{:S(2)}) collective-permute-start(bf16[96,896]{1,0:T(8,128)(2,1)S(1)} %shard_map.418.refs_5_), channel_id=1, source_target_pairs={{0,16},{4,20},{8,24},{12,28},{16,0},{20,4},{24,8},{28,12},{1,17},{... | collective-permute-start | bytes 516104 | tf_op jit(solution)/shard_map/ppermute | solution.py:669
  57.4 14.5 %collective-permute-start.16 = (bf16[96,896]{1,0:T(8,128)(2,1)S(1)}, bf16[96,896]{1,0:T(8,128)(2,1)S(1)}, u32[]{:S(2)}, u32[]{:S(2)}) collective-permute-start(bf16[96,896]{1,0:T(8,128)(2,1)S(1)} %shard_map.418.refs_5_), channel_id=1, source_target_pairs={{0,8},{4,12},{8,0},{12,4},{16,24},{20,28},{24,16},{28,20},{1,9},{5... | collective-permute-start | bytes 516104 | tf_op jit(solution)/shard_map/ppermute | solution.py:669
  58.0 14.3 %collective-permute-start.15 = (bf16[96,896]{1,0:T(8,128)(2,1)S(1)}, bf16[96,896]{1,0:T(8,128)(2,1)S(1)}, u32[]{:S(2)}, u32[]{:S(2)}) collective-permute-start(bf16[96,896]{1,0:T(8,128)(2,1)S(1)} %shard_map.418.refs_5_), channel_id=1, source_target_pairs={{0,4},{4,0},{8,12},{12,8},{16,20},{20,16},{24,28},{28,24},{1,5},{5... | collective-permute-start | bytes 516104 | tf_op jit(solution)/shard_map/ppermute | solution.py:669
  62.7 19.7 %collective-permute-start.12 = (bf16[128,768]{1,0:T(8,128)(2,1)S(1)}, bf16[128,768]{1,0:T(8,128)(2,1)S(1)}, u32[]{:S(2)}, u32[]{:S(2)}) collective-permute-start(bf16[128,768]{1,0:T(8,128)(2,1)S(1)} %get-tuple-element.103.refs_0_), channel_id=1, source_target_pairs={{0,1},{1,0},{2,3},{3,2},{4,5},{5,4},{6,7},{7,6},{8,9},{9,8},{10,11... | collective-permute-start | bytes 589832 | tf_op jit(solution)/shard_map/ppermute | solution.py:666
  62.7 19.7 %collective-permute-start.14 = (bf16[128,768]{1,0:T(8,128)(2,1)S(1)}, bf16[128,768]{1,0:T(8,128)(2,1)S(1)}, u32[]{:S(2)}, u32[]{:S(2)}) collective-permute-start(bf16[128,768]{1,0:T(8,128)(2,1)S(1)} %collective-permute-done.13.refs_2_), channel_id=1, source_target_pairs={{0,1},{1,0},{2,3},{3,2},{4,5},{5,4},{6,7},{7,6},{8,9},{9,8},{10,11... | collective-permute-start | bytes 589832 | tf_op jit(solution)/shard_map/ppermute | solution.py:666
  71.9 8.7 %collective-permute-start.19 = (bf16[96,896]{1,0:T(8,128)(2,1)S(1)}, bf16[96,896]{1,0:T(8,128)(2,1)S(1)}, u32[]{:S(2)}, u32[]{:S(2)}) collective-permute-start(bf16[96,896]{1,0:T(8,128)(2,1)S(1)} %collective-permute-done.18.refs_9_), channel_id=1, source_target_pairs={{0,4},{4,0},{8,12},{12,8},{16,20},{20,16},{24,28},{28,24},{1,5},{5... | collective-permute-start | bytes 516104 | tf_op jit(solution)/shard_map/ppermute | solution.py:669
  72.4 10.0 %collective-permute-start.17 = (bf16[96,896]{1,0:T(8,128)(2,1)S(1)}, bf16[96,896]{1,0:T(8,128)(2,1)S(1)}, u32[]{:S(2)}, u32[]{:S(2)}) collective-permute-start(bf16[96,896]{1,0:T(8,128)(2,1)S(1)} %collective-permute-done.16.refs_7_), channel_id=1, source_target_pairs={{0,4},{4,0},{8,12},{12,8},{16,20},{20,16},{24,28},{28,24},{1,5},{5... | collective-permute-start | bytes 516104 | tf_op jit(solution)/shard_map/ppermute | solution.py:669
  97.6 14.2 %collective-permute-start.36 = (bf16[2,96,896]{2,1,0:T(8,128)(2,1)S(1)}, bf16[2,96,896]{2,1,0:T(8,128)(2,1)S(1)}, u32[]{:S(2)}, u32[]{:S(2)}) collective-permute-start(bf16[2,96,896]{2,1,0:T(8,128)(2,1)S(1)} %get-tuple-element.139), channel_id=1, source_target_pairs={{0,8},{4,12},{8,0},{12,4},{16,24},{20,28},{24,16},{28,20},{1,9},{5... | collective-permute-start | bytes 1032200 | tf_op jit(solution)/shard_map/ppermute | solution.py:669
  101.2 21.6 %collective-permute-start.29 = (bf16[2,128,768]{2,1,0:T(8,128)(2,1)S(1)}, bf16[2,128,768]{2,1,0:T(8,128)(2,1)S(1)}, u32[]{:S(2)}, u32[]{:S(2)}) collective-permute-start(bf16[2,128,768]{2,1,0:T(8,128)(2,1)S(1)} %get-tuple-element.122), channel_id=1, source_target_pairs={{0,1},{1,0},{2,3},{3,2},{4,5},{5,4},{6,7},{7,6},{8,9},{9,8},{10,11... | collective-permute-start | bytes 1179656 | tf_op jit(solution)/shard_map/ppermute | solution.py:666
  101.7 18.3 %collective-permute-start.37 = (bf16[2,96,896]{2,1,0:T(8,128)(2,1)S(1)}, bf16[2,96,896]{2,1,0:T(8,128)(2,1)S(1)}, u32[]{:S(2)}, u32[]{:S(2)}) collective-permute-start(bf16[2,96,896]{2,1,0:T(8,128)(2,1)S(1)} %get-tuple-element.140), channel_id=1, source_target_pairs={{0,16},{4,20},{8,24},{12,28},{16,0},{20,4},{24,8},{28,12},{1,17},{... | collective-permute-start | bytes 1032200 | tf_op jit(solution)/shard_map/ppermute | solution.py:669
  101.7 8.7 %collective-permute-start.39 = (bf16[96,896]{1,0:T(8,128)(2,1)S(1)}, bf16[96,896]{1,0:T(8,128)(2,1)S(1)}, u32[]{:S(2)}, u32[]{:S(2)}) collective-permute-start(bf16[96,896]{1,0:T(8,128)(2,1)S(1)} %get-tuple-element.144), channel_id=1, source_target_pairs={{0,4},{4,0},{8,12},{12,8},{16,20},{20,16},{24,28},{28,24},{1,5},{5... | collective-permute-start | bytes 516104 | tf_op jit(solution)/shard_map/ppermute | solution.py:669
  110.3 14.1 %collective-permute-start.27 = (bf16[2,128,768]{2,1,0:T(8,128)(2,1)S(1)}, bf16[2,128,768]{2,1,0:T(8,128)(2,1)S(1)}, u32[]{:S(2)}, u32[]{:S(2)}) collective-permute-start(bf16[2,128,768]{2,1,0:T(8,128)(2,1)S(1)} %get-tuple-element.118), channel_id=1, source_target_pairs={{0,1},{1,0},{2,3},{3,2},{4,5},{5,4},{6,7},{7,6},{8,9},{9,8},{10,11... | collective-permute-start | bytes 1179656 | tf_op jit(solution)/shard_map/ppermute | solution.py:666
  110.4 14.7 %collective-permute-start.31 = (bf16[2,96,768]{2,1,0:T(8,128)(2,1)S(1)}, bf16[2,96,768]{2,1,0:T(8,128)(2,1)S(1)}, u32[]{:S(2)}, u32[]{:S(2)}) collective-permute-start(bf16[2,96,768]{2,1,0:T(8,128)(2,1)S(1)} %get-tuple-element.128), channel_id=1, source_target_pairs={{0,4},{4,0},{8,12},{12,8},{16,20},{20,16},{24,28},{28,24},{1,5},{5... | collective-permute-start | bytes 884744 | tf_op jit(solution)/shard_map/ppermute | solution.py:669
  111.8 15.0 %collective-permute-start.33 = (bf16[2,96,768]{2,1,0:T(8,128)(2,1)S(1)}, bf16[2,96,768]{2,1,0:T(8,128)(2,1)S(1)}, u32[]{:S(2)}, u32[]{:S(2)}) collective-permute-start(bf16[2,96,768]{2,1,0:T(8,128)(2,1)S(1)} %get-tuple-element.132), channel_id=1, source_target_pairs={{0,4},{4,0},{8,12},{12,8},{16,20},{20,16},{24,28},{28,24},{1,5},{5... | collective-permute-start | bytes 884744 | tf_op jit(solution)/shard_map/ppermute | solution.py:669
  120.0 9.8 %collective-permute-start.40 = (bf16[96,896]{1,0:T(8,128)(2,1)S(1)}, bf16[96,896]{1,0:T(8,128)(2,1)S(1)}, u32[]{:S(2)}, u32[]{:S(2)}) collective-permute-start(bf16[96,896]{1,0:T(8,128)(2,1)S(1)} %shard_map.431), channel_id=1, source_target_pairs={{0,24},{4,28},{8,16},{12,20},{16,8},{20,12},{24,0},{28,4},{1,25},{... | collective-permute-start | bytes 516104 | tf_op jit(solution)/shard_map/ppermute | solution.py:669
  122.8 7.8 %collective-permute-start.38 = (bf16[96,896]{1,0:T(8,128)(2,1)S(1)}, bf16[96,896]{1,0:T(8,128)(2,1)S(1)}, u32[]{:S(2)}, u32[]{:S(2)}) collective-permute-start(bf16[96,896]{1,0:T(8,128)(2,1)S(1)} %get-tuple-element.142), channel_id=1, source_target_pairs={{0,4},{4,0},{8,12},{12,8},{16,20},{20,16},{24,28},{28,24},{1,5},{5... | collective-permute-start | bytes 516104 | tf_op jit(solution)/shard_map/ppermute | solution.py:669
  124.5 23.3 %collective-permute-start.30 = (bf16[128,768]{1,0:T(8,128)(2,1)S(1)}, bf16[128,768]{1,0:T(8,128)(2,1)S(1)}, u32[]{:S(2)}, u32[]{:S(2)}) collective-permute-start(bf16[128,768]{1,0:T(8,128)(2,1)S(1)} %get-tuple-element.124), channel_id=1, source_target_pairs={{0,2},{1,3},{2,0},{3,1},{4,6},{5,7},{6,4},{7,5},{8,10},{9,11},{10,... | collective-permute-start | bytes 589832 | tf_op jit(solution)/shard_map/ppermute | solution.py:666
  125.2 22.6 %collective-permute-start.28 = (bf16[128,768]{1,0:T(8,128)(2,1)S(1)}, bf16[128,768]{1,0:T(8,128)(2,1)S(1)}, u32[]{:S(2)}, u32[]{:S(2)}) collective-permute-start(bf16[128,768]{1,0:T(8,128)(2,1)S(1)} %get-tuple-element.120), channel_id=1, source_target_pairs={{0,2},{1,3},{2,0},{3,1},{4,6},{5,7},{6,4},{7,5},{8,10},{9,11},{10,... | collective-permute-start | bytes 589832 | tf_op jit(solution)/shard_map/ppermute | solution.py:666
  126.8 8.0 %collective-permute-start.32 = (bf16[96,768]{1,0:T(8,128)(2,1)S(1)}, bf16[96,768]{1,0:T(8,128)(2,1)S(1)}, u32[]{:S(2)}, u32[]{:S(2)}) collective-permute-start(bf16[96,768]{1,0:T(8,128)(2,1)S(1)} %get-tuple-element.130), channel_id=1, source_target_pairs={{0,8},{4,12},{8,0},{12,4},{16,24},{20,28},{24,16},{28,20},{1,9},{5... | collective-permute-start | bytes 442376 | tf_op jit(solution)/shard_map/ppermute | solution.py:669
  129.8 12.8 %collective-permute-start.34 = (bf16[96,768]{1,0:T(8,128)(2,1)S(1)}, bf16[96,768]{1,0:T(8,128)(2,1)S(1)}, u32[]{:S(2)}, u32[]{:S(2)}) collective-permute-start(bf16[96,768]{1,0:T(8,128)(2,1)S(1)} %get-tuple-element.133), channel_id=1, source_target_pairs={{0,16},{4,20},{8,24},{12,28},{16,0},{20,4},{24,8},{28,12},{1,17},{... | collective-permute-start | bytes 442376 | tf_op jit(solution)/shard_map/ppermute | solution.py:669
  130.6 12.0 %collective-permute-start.35 = (bf16[96,768]{1,0:T(8,128)(2,1)S(1)}, bf16[96,768]{1,0:T(8,128)(2,1)S(1)}, u32[]{:S(2)}, u32[]{:S(2)}) collective-permute-start(bf16[96,768]{1,0:T(8,128)(2,1)S(1)} %get-tuple-element.134), channel_id=1, source_target_pairs={{0,24},{4,28},{8,16},{12,20},{16,8},{20,12},{24,0},{28,4},{1,25},{... | collective-permute-start | bytes 442376 | tf_op jit(solution)/shard_map/ppermute | solution.py:669
  (36 other events, 289.7 us)
where the time goes:
time: 149 us
  waiting for transfers between devices  70.5 us (47%)
  starting transfers between devices  50.9 us (34%)
  Pallas kernels  24.4 us (16%)
  local copies, waits for them, and re-layouts  2.11 us (1%)
    ppermute x24, waiting for transfers between devices, over_dp(): return lax.ppermute(value, 'dp', [(i, i ^ step) for i in range(dp)])  46.5 us
    ppermute x24, starting transfers between devices, over_dp(): return lax.ppermute(value, 'dp', [(i, i ^ step) for i in range(dp)])  38.2 us
    pallas_call x23, Pallas kernels, run_kernel(): pl.pallas_call(body, out_shape=out_shape, in_specs=in_specs, out_specs=[p...  24.4 us
    ppermute x20, waiting for transfers between devices, over_mp(): return lax.ppermute(value, 'mp', [(i, i ^ step) for i in range(mp)])  24 us
    ppermute x20, starting transfers between devices, over_mp(): return lax.ppermute(value, 'mp', [(i, i ^ step) for i in range(mp)])  12.6 us
  transfers between devices with their start and end apart: 44, of which 19 were waited for; matrix products, arithmetic and copies ran while one was open for 0% of the time, Pallas kernels for 9%

commit v1 on v0

--- a/solution.py
+++ b/solution.py
@@ -31,13 +31,13 @@
 BF16 = jnp.bfloat16
 
 
-def run_kernel(body, outs, args, scalars=0, scratch=(), limit=24, final=False):
+def run_kernel(body, outs, args, scalars=0, scratch=(), limit=24, final=False, space=pltpu.VMEM):
     in_specs = [pl.BlockSpec(memory_space=pltpu.SMEM)] * scalars
-    in_specs += [pl.BlockSpec(memory_space=pltpu.VMEM)] * (len(args) - scalars)
+    in_specs += [pl.BlockSpec(memory_space=space)] * (len(args) - scalars)
     out_shape = [jax.ShapeDtypeStruct(shape, kind) for shape, kind in outs]
     if not INTERPRET:
         args = args[:scalars] + tuple(
-            pltpu.with_memory_space_constraint(item, pltpu.VMEM) for item in args[scalars:]
+            pltpu.with_memory_space_constraint(item, space) for item in args[scalars:]
         )
         if not final:
             out_shape = [pltpu.VMEM(shape, kind) for shape, kind in outs]
@@ -279,22 +279,30 @@
     return body
 
 
+def group_steps(chunks):
+    count = chunks // 2
+    return [tuple(range(count - 2))] + [(count - 2,), (count - 1,)]
+
+
 def spread_chunks(grad, spots, outs, deep, chunks):
     if chunks == 1:
         outs[0][...] = grad[...]
         return
-    group = outs[0].shape[0]
-    for i in range(chunks // 2):
-        mine, send = outs[2 * (i // group)], outs[2 * (i // group) + 1]
-        mine[i % group] = grad[at_block(spots, 2 * i, deep), :]
-        send[i % group] = grad[at_block(spots, 2 * i + 1, deep), :].astype(BF16)
-
-
-def chunk_outs(chunks, deep, lanes, groups):
+    for g, steps in enumerate(group_steps(chunks)):
+        mine, send = outs[2 * g], outs[2 * g + 1]
+        for place, i in enumerate(steps):
+            mine[place] = grad[at_block(spots, 2 * i, deep), :]
+            send[place] = grad[at_block(spots, 2 * i + 1, deep), :].astype(BF16)
+
+
+def chunk_outs(chunks, deep, lanes):
     if chunks == 1:
         return [((deep, lanes), F32)]
-    shape = (chunks // 2 // groups, deep, lanes)
-    return [(shape, F32), (shape, BF16)] * groups
+    outs = []
+    for steps in group_steps(chunks):
+        shape = (len(steps), deep, lanes)
+        outs += [(shape, F32), (shape, BF16)]
+    return outs
 
 
 def chunk_sum_kernel(mine_ref, got_ref, *outs):
@@ -306,11 +314,12 @@
     if chunks == 1:
         outs[0][...] = grad[...]
         return
-    for i, out in enumerate(outs[:-2]):
+    steps = [i for i in range(chunks // 2) if i != chunks // 2 - 2]
+    for i, out in zip(steps, outs):
         for side in range(2):
             out[side] = grad[at_block(spots, 2 * i + side, deep), :].astype(out.dtype)
-    outs[-2][...] = grad[at_block(spots, chunks - 2, deep), :]
-    outs[-1][...] = grad[at_block(spots, chunks - 1, deep), :].astype(BF16)
+    outs[-2][...] = grad[at_block(spots, chunks - 4, deep), :]
+    outs[-1][...] = grad[at_block(spots, chunks - 3, deep), :].astype(BF16)
 
 
 def pair_outs(chunks, deep, lanes):
@@ -476,7 +485,17 @@
     return value.astype(BF16).astype(F32)
 
 
-def pack_attend_kernel(gain_ref, triple_ref, merge_ref, out_ref):
+def pack_attend_kernel(gain_far, triple_far, merge_far, out_ref, gain_ref, triple_ref, merge_ref, sems):
+    pairs = [(gain_far, gain_ref), (merge_far, merge_ref)]
+    pairs += [(triple_far.at[c], triple_ref.at[c]) for c in range(3)]
+    copies = [
+        pltpu.make_async_copy(source, target, sems.at[i])
+        for i, (source, target) in enumerate(pairs)
+    ]
+    for copy in copies:
+        copy.start()
+    for copy in copies:
+        copy.wait()
     gain = column_of(rounded(gain_ref[...]))
     q, k, v = (rounded(triple_ref[c]) * gain for c in range(3))
     merge = merge_ref[...].T
@@ -678,29 +697,25 @@
     def reduce_chunks(chunks):
         if not direct:
             return [lax.psum_scatter(chunks[0], "dp", scatter_dimension=0, tiled=True)]
-        groups = len(chunks) // 2
         found = []
-        for g in range(groups):
+        for g, steps in enumerate(group_steps(dp)):
             mine, send = chunks[2 * g], chunks[2 * g + 1]
             got = over_dp(send, 1)
-            first = g * mine.shape[0]
-            outs = [
-                (mine.shape[1:], BF16 if first + i else F32) for i in range(mine.shape[0])
-            ]
+            outs = [(mine.shape[1:], BF16 if i else F32) for i in steps]
             sums = run_kernel(chunk_sum_kernel, outs, (mine, got))
-            for i, part in enumerate(sums):
-                step = 2 * (first + i)
-                found.append(over_dp(part, step) if step else part)
+            for i, part in zip(steps, sums):
+                found.append(over_dp(part, 2 * i) if i else part)
         return found
 
     def reduce_pairs(pairs):
         if not direct:
             return [lax.psum_scatter(pairs[0], "dp", scatter_dimension=0, tiled=True)]
-        got = [over_dp(pairs[i], 2 * i) for i in range(1, dp // 2 - 1)]
+        steps = [i for i in range(1, dp // 2) if i != dp // 2 - 2]
+        got = [over_dp(pair, 2 * i) for i, pair in zip(steps, pairs[1:])]
         mine, send = pairs[-2:]
         shape = mine.shape
         (last,) = run_kernel(near_sum_kernel, [(shape, BF16)], (mine, over_dp(send, 1)))
-        last = over_dp(last, dp - 2)
+        last = over_dp(last, dp - 4)
         mine, send = run_kernel(pair_sum_kernel, [(shape, F32), (shape, BF16)], (pairs[0], *got))
         return [mine, over_dp(send, 1), last]
 
@@ -738,6 +753,11 @@
                 pack_attend_kernel,
                 [((deep, 6 * LANES), BF16)],
                 (gain_row, weight_triple, weight_merge),
+                scratch=[
+                    pltpu.VMEM(item.shape, F32) for item in (gain_row, weight_triple, weight_merge)
+                ]
+                + [pltpu.SemaphoreType.DMA((5,))],
+                space=pltpu.HBM,
             )
             (second_pack,) = run_kernel(
                 pack_feed_kernel,
@@ -824,7 +844,7 @@
         feed_parts = reduce_pairs(feed_chunks)
         d_pre, *attend_chunks = run_kernel(
             make_attend_back(length, width, rows, chunks),
-            [((length, 5 * LANES), BF16)] + chunk_outs(chunks, deep, 6 * LANES, 2),
+            [((length, 5 * LANES), BF16)] + chunk_outs(chunks, deep, 6 * LANES),
             (places, spots, cosine, sine, *blocks, normed, weight, qkv, att, lse),
             scalars=2,
             scratch=[

time: 149 us -> 161 us (1.081)
  waiting for transfers between devices: 70.5 us -> 83.4 us
  starting transfers between devices: 50.9 us -> 48.6 us
    ppermute x24 -> x25, waiting for transfers between devices: 46.5 us -> 57.2 us  [over_dp(): return lax.ppermute(value, 'dp', [(i, i ^ step) for i in range(dp)])]
    ppermute x20, waiting for transfers between devices: 24 us -> 26.2 us  [over_mp(): return lax.ppermute(value, 'mp', [(i, i ^ step) for i in range(mp)])]
    ppermute x24 -> x25, starting transfers between devices: 38.2 us -> 36.9 us  [over_dp(): return lax.ppermute(value, 'dp', [(i, i ^ step) for i in range(dp)])]
    pallas_call x23 -> x24, Pallas kernels: 24.4 us -> 25.6 us  [run_kernel(): pl.pallas_call(body, out_shape=out_shape, in_specs=in_specs, out_specs=[p...]
  transfers between devices with their start and end apart: 44 -> 45, of which waited for: 19 -> 23; matrix products, arithmetic and copies ran while one was open for 0% -> 0% of each run, Pallas kernels for 9% -> 9%
where the time goes in v1:
time: 161 us
  waiting for transfers between devices  83.4 us (52%)
  starting transfers between devices  48.6 us (30%)
  Pallas kernels  25.6 us (16%)
  local copies, waits for them, and re-layouts  2.12 us (1%)
    ppermute x25, waiting for transfers between devices, over_dp(): return lax.ppermute(value, 'dp', [(i, i ^ step) for i in range(dp)])  57.2 us
    ppermute x25, starting transfers between devices, over_dp(): return lax.ppermute(value, 'dp', [(i, i ^ step) for i in range(dp)])  36.9 us
    ppermute x20, waiting for transfers between devices, over_mp(): return lax.ppermute(value, 'mp', [(i, i ^ step) for i in range(mp)])  26.2 us
    pallas_call x24, Pallas kernels, run_kernel(): pl.pallas_call(body, out_shape=out_shape, in_specs=in_specs, out_specs=[p...  25.6 us
    ppermute x20, starting transfers between devices, over_mp(): return lax.ppermute(value, 'mp', [(i, i ^ step) for i in range(mp)])  11.7 us
  transfers between devices with their start and end apart: 45, of which 23 were waited for; matrix products, arithmetic and copies ran while one was open for 0% of the time, Pallas kernels for 9%

profile of v1, /device:TPU:0, one launch (start us, length us, event | category | flops | bytes accessed | tf_op | source)
XLA Modules:
  0.0 160.8 jit_solution(7514866528440830454)
XLA Ops:
  3.5 3.0 %collective-permute-start.1 = (bf16[128,1536]{1,0:T(8,128)(2,1)S(1)}, bf16[128,1536]{1,0:T(8,128)(2,1)S(1)}, u32[]{:S(2)}, u32[]{:S(2)}) collective-permute-start(bf16[128,1536]{1,0:T(8,128)(2,1)S(1)} %shard_map.413.refs_0_), channel_id=1, source_target_pairs={{0,2},{1,3},{2,0},{3,1},{4,6},{5,7},{6,4},{7,5},{8,10},{9,11},{10,... | collective-permute-start | bytes 1179656 | tf_op jit(solution)/shard_map/ppermute | solution.py:685
  7.8 3.7 %collective-permute-start.8 = (bf16[96,768]{1,0:T(8,128)(2,1)S(1)}, bf16[96,768]{1,0:T(8,128)(2,1)S(1)}, u32[]{:S(2)}, u32[]{:S(2)}) collective-permute-start(bf16[96,768]{1,0:T(8,128)(2,1)S(1)} %shard_map.414.refs_4_), channel_id=1, source_target_pairs={{0,24},{4,28},{8,16},{12,20},{16,8},{20,12},{24,0},{28,4},{1,25},{... | collective-permute-start | bytes 442376 | tf_op jit(solution)/shard_map/ppermute | solution.py:688
  11.5 4.1 %collective-permute-done.1.refs_2_ = bf16[128,1536]{1,0:T(8,128)(2,1)S(1)} collective-permute-done((bf16[128,1536]{1,0:T(8,128)(2,1)S(1)}, bf16[128,1536]{1,0:T(8,128)(2,1)S(1)}, u32[]{:S(2)}, u32[]{:S(2)}) %collective-permute-start.1) | collective-permute-done | bytes 393248 | tf_op jit(solution)/shard_map/ppermute | solution.py:685
  15.6 2.8 %collective-permute-start.6 = (bf16[96,768]{1,0:T(8,128)(2,1)S(1)}, bf16[96,768]{1,0:T(8,128)(2,1)S(1)}, u32[]{:S(2)}, u32[]{:S(2)}) collective-permute-start(bf16[96,768]{1,0:T(8,128)(2,1)S(1)} %shard_map.414.refs_4_), channel_id=1, source_target_pairs={{0,16},{4,20},{8,24},{12,28},{16,0},{20,4},{24,8},{28,12},{1,17},{... | collective-permute-start | bytes 442376 | tf_op jit(solution)/shard_map/ppermute | solution.py:688
  21.6 4.7 %collective-permute-done.6.refs_8_ = bf16[96,768]{1,0:T(8,128)(2,1)S(1)} collective-permute-done((bf16[96,768]{1,0:T(8,128)(2,1)S(1)}, bf16[96,768]{1,0:T(8,128)(2,1)S(1)}, u32[]{:S(2)}, u32[]{:S(2)}) %collective-permute-start.6) | collective-permute-done | bytes 147488 | tf_op jit(solution)/shard_map/ppermute | solution.py:688
  29.8 3.1 %collective-permute-done.9.refs_11_ = bf16[96,768]{1,0:T(8,128)(2,1)S(1)} collective-permute-done((bf16[96,768]{1,0:T(8,128)(2,1)S(1)}, bf16[96,768]{1,0:T(8,128)(2,1)S(1)}, u32[]{:S(2)}, u32[]{:S(2)}) %collective-permute-start.9) | collective-permute-done | bytes 147488 | tf_op jit(solution)/shard_map/ppermute | solution.py:688
  33.0 3.2 %collective-permute-done.7.refs_9_ = bf16[96,768]{1,0:T(8,128)(2,1)S(1)} collective-permute-done((bf16[96,768]{1,0:T(8,128)(2,1)S(1)}, bf16[96,768]{1,0:T(8,128)(2,1)S(1)}, u32[]{:S(2)}, u32[]{:S(2)}) %collective-permute-start.7) | collective-permute-done | bytes 147488 | tf_op jit(solution)/shard_map/ppermute | solution.py:688
  36.1 2.0 %collective-permute-done.5.refs_7_ = bf16[96,768]{1,0:T(8,128)(2,1)S(1)} collective-permute-done((bf16[96,768]{1,0:T(8,128)(2,1)S(1)}, bf16[96,768]{1,0:T(8,128)(2,1)S(1)}, u32[]{:S(2)}, u32[]{:S(2)}) %collective-permute-start.5) | collective-permute-done | bytes 147488 | tf_op jit(solution)/shard_map/ppermute | solution.py:688
  38.1 4.5 %shard_map.415 = (bf16[512,768]{1,0:T(8,128)(2,1)S(1)}, bf16[512,768]{1,0:T(8,128)(2,1)S(1)}, bf16[768,768]{1,0:T(8,128)(2,1)S(1)}, bf16[512,640]{1,0:T(8,128)(2...) custom-call(s32[4]{0:T(128)S(1)} %xor_multiply_fusion.1.places, ...), custom_call_target="tpu_custom_call" | custom-call | tf_op jit(solution)/shard_map/pallas_call | solution.py:44
  42.8 1.7 %collective-permute-done.10.got_ref = bf16[2,128,768]{2,1,0:T(8,128)(2,1)S(1)} collective-permute-done((bf16[2,128,768]{2,1,0:T(8,128)(2,1)S(1)}, bf16[2,128,768]{2,1,0:T(8,128)(2,1)S(1)}, u32[]{:S(2)}, u32[]{:S(2)}) %collective-permute-start.10) | collective-permute-done | bytes 393248 | tf_op jit(solution)/shard_map/ppermute | solution.py:685
  46.0 5.6 %collective-permute-done.11.got_ref = bf16[128,768]{1,0:T(8,128)(2,1)S(1)} collective-permute-done((bf16[128,768]{1,0:T(8,128)(2,1)S(1)}, bf16[128,768]{1,0:T(8,128)(2,1)S(1)}, u32[]{:S(2)}, u32[]{:S(2)}) %collective-permute-start.11) | collective-permute-done | bytes 196640 | tf_op jit(solution)/shard_map/ppermute | solution.py:685
  53.5 3.9 %collective-permute-start.20 = (bf16[96,896]{1,0:T(8,128)(2,1)S(1)}, bf16[96,896]{1,0:T(8,128)(2,1)S(1)}, u32[]{:S(2)}, u32[]{:S(2)}) collective-permute-start(bf16[96,896]{1,0:T(8,128)(2,1)S(1)} %shard_map.418.refs_5_), channel_id=1, source_target_pairs={{0,24},{4,28},{8,16},{12,20},{16,8},{20,12},{24,0},{28,4},{1,25},{... | collective-permute-start | bytes 516104 | tf_op jit(solution)/shard_map/ppermute | solution.py:688
  59.5 3.1 %collective-permute-done.20.refs_11_ = bf16[96,896]{1,0:T(8,128)(2,1)S(1)} collective-permute-done((bf16[96,896]{1,0:T(8,128)(2,1)S(1)}, bf16[96,896]{1,0:T(8,128)(2,1)S(1)}, u32[]{:S(2)}, u32[]{:S(2)}) %collective-permute-start.20) | collective-permute-done | bytes 172064 | tf_op jit(solution)/shard_map/ppermute | solution.py:688
  63.2 7.2 %collective-permute-done.18.refs_9_ = bf16[96,896]{1,0:T(8,128)(2,1)S(1)} collective-permute-done((bf16[96,896]{1,0:T(8,128)(2,1)S(1)}, bf16[96,896]{1,0:T(8,128)(2,1)S(1)}, u32[]{:S(2)}, u32[]{:S(2)}) %collective-permute-start.18) | collective-permute-done | bytes 172064 | tf_op jit(solution)/shard_map/ppermute | solution.py:688
  73.9 3.7 %collective-permute-done.21.refs_12_ = bf16[96,896]{1,0:T(8,128)(2,1)S(1)} collective-permute-done((bf16[96,896]{1,0:T(8,128)(2,1)S(1)}, bf16[96,896]{1,0:T(8,128)(2,1)S(1)}, u32[]{:S(2)}, u32[]{:S(2)}) %collective-permute-start.21) | collective-permute-done | bytes 172064 | tf_op jit(solution)/shard_map/ppermute | solution.py:688
  77.6 2.9 %collective-permute-done.19.refs_10_ = bf16[96,896]{1,0:T(8,128)(2,1)S(1)} collective-permute-done((bf16[96,896]{1,0:T(8,128)(2,1)S(1)}, bf16[96,896]{1,0:T(8,128)(2,1)S(1)}, u32[]{:S(2)}, u32[]{:S(2)}) %collective-permute-start.19) | collective-permute-done | bytes 172064 | tf_op jit(solution)/shard_map/ppermute | solution.py:688
  80.5 1.8 %collective-permute-done.17.refs_8_ = bf16[96,896]{1,0:T(8,128)(2,1)S(1)} collective-permute-done((bf16[96,896]{1,0:T(8,128)(2,1)S(1)}, bf16[96,896]{1,0:T(8,128)(2,1)S(1)}, u32[]{:S(2)}, u32[]{:S(2)}) %collective-permute-start.17) | collective-permute-done | bytes 172064 | tf_op jit(solution)/shard_map/ppermute | solution.py:688
  82.4 3.4 %shard_map.419 = (bf16[512,768]{1,0:T(8,128)(2,1)S(1)}, bf16[512,640]{1,0:T(8,128)(2,1)S(1)}, bf16[512,384]{1,0:T(8,128)(2,1)S(1)}, f32[2,128,768]{2,1,0:T(8,128...) custom-call(s32[4]{0:T(128)S(1)} %xor_multiply_fusion.1.places, ...), custom_call_target="tpu_custom_call" | custom-call | tf_op jit(solution)/shard_map/pallas_call | solution.py:44
  85.9 1.7 %collective-permute-done.22.got_ref = bf16[2,128,768]{2,1,0:T(8,128)(2,1)S(1)} collective-permute-done((bf16[2,128,768]{2,1,0:T(8,128)(2,1)S(1)}, bf16[2,128,768]{2,1,0:T(8,128)(2,1)S(1)}, u32[]{:S(2)}, u32[]{:S(2)}) %collective-permute-start.22) | collective-permute-done | bytes 393248 | tf_op jit(solution)/shard_map/ppermute | solution.py:685
  88.3 6.4 %collective-permute-done.23.got_ref = bf16[128,768]{1,0:T(8,128)(2,1)S(1)} collective-permute-done((bf16[128,768]{1,0:T(8,128)(2,1)S(1)}, bf16[128,768]{1,0:T(8,128)(2,1)S(1)}, u32[]{:S(2)}, u32[]{:S(2)}) %collective-permute-start.23) | collective-permute-done | bytes 196640 | tf_op jit(solution)/shard_map/ppermute | solution.py:685
  95.6 5.6 %collective-permute-done.25.refs_2_ = bf16[128,768]{1,0:T(8,128)(2,1)S(1)} collective-permute-done((bf16[128,768]{1,0:T(8,128)(2,1)S(1)}, bf16[128,768]{1,0:T(8,128)(2,1)S(1)}, u32[]{:S(2)}, u32[]{:S(2)}) %collective-permute-start.25) | collective-permute-done | bytes 196640 | tf_op jit(solution)/shard_map/ppermute | solution.py:685
  102.6 5.7 %shard_map.422 = (bf16[512,640]{1,0:T(8,128)(2,1)S(1)}, f32[2,96,768]{2,1,0:T(8,128)S(1)}, bf16[2,96,768]{2,1,0:T(8,128)(2,1)S(1)}, f32[1,96,768]{2,1,0:T(8,128)...) custom-call(s32[4]{0:T(128)S(1)} %xor_multiply_fusion.1.places, ...), custom_call_target="tpu_custom_call" | custom-call | tf_op jit(solution)/shard_map/pallas_call | solution.py:44
  109.9 1.9 %shard_map.430 = (f32[2,96,896]{2,1,0:T(8,128)S(1)}, bf16[2,96,896]{2,1,0:T(8,128)(2,1)S(1)}, bf16[2,96,896]{2,1,0:T(8,128)(2,1)S(1)}, f32[96,896]{1,0:T(8,128)S(1)}, bf16[96,896]{1,0:T(8,128)(2,1)S(1)}) custom-call(s32[8]{0:T(128)S(1)} %xor_multiply_fusion.spots, bf16[512,768]{1,0:T(8,128)(2,1)S(1)} %get-tuple-element.135.normed, ...), custom_call_target="tpu_custom_call" | custom-call | tf_op jit(solution)/shard_map/pallas_call | solution.py:44
  116.0 4.8 %collective-permute-done.40.got = bf16[96,896]{1,0:T(8,128)(2,1)S(1)} collective-permute-done((bf16[96,896]{1,0:T(8,128)(2,1)S(1)}, bf16[96,896]{1,0:T(8,128)(2,1)S(1)}, u32[]{:S(2)}, u32[]{:S(2)}) %collective-permute-start.40) | collective-permute-done | bytes 172064 | tf_op jit(solution)/shard_map/ppermute | solution.py:688
  123.8 6.6 %collective-permute-done.38.refs_2_ = bf16[2,96,896]{2,1,0:T(8,128)(2,1)S(1)} collective-permute-done((bf16[2,96,896]{2,1,0:T(8,128)(2,1)S(1)}, bf16[2,96,896]{2,1,0:T(8,128)(2,1)S(1)}, u32[]{:S(2)}, u32[]{:S(2)}) %collective-permute-start.38) | collective-permute-done | bytes 344096 | tf_op jit(solution)/shard_map/ppermute | solution.py:688
  132.1 2.0 %collective-permute-start.41 = (bf16[96,896]{1,0:T(8,128)(2,1)S(1)}, bf16[96,896]{1,0:T(8,128)(2,1)S(1)}, u32[]{:S(2)}, u32[]{:S(2)}) collective-permute-start(bf16[96,896]{1,0:T(8,128)(2,1)S(1)} %shard_map.432), channel_id=1, source_target_pairs={{0,16},{4,20},{8,24},{12,28},{16,0},{20,4},{24,8},{28,12},{1,17},{... | collective-permute-start | bytes 516104 | tf_op jit(solution)/shard_map/ppermute | solution.py:688
  135.4 1.7 %collective-permute-done.35.got_ref = bf16[1,96,768]{2,1,0:T(8,128)(2,1)S(1)} collective-permute-done((bf16[1,96,768]{2,1,0:T(8,128)(2,1)S(1)}, bf16[1,96,768]{2,1,0:T(8,128)(2,1)S(1)}, u32[]{:S(2)}, u32[]{:S(2)}) %collective-permute-start.35) | collective-permute-done | bytes 147488 | tf_op jit(solution)/shard_map/ppermute | solution.py:688
  138.9 6.5 %collective-permute-done.41.refs_2_ = bf16[96,896]{1,0:T(8,128)(2,1)S(1)} collective-permute-done((bf16[96,896]{1,0:T(8,128)(2,1)S(1)}, bf16[96,896]{1,0:T(8,128)(2,1)S(1)}, u32[]{:S(2)}, u32[]{:S(2)}) %collective-permute-start.41) | collective-permute-done | bytes 172064 | tf_op jit(solution)/shard_map/ppermute | solution.py:688
  145.3 1.9 %collective-permute-start.36 = (bf16[96,768]{1,0:T(8,128)(2,1)S(1)}, bf16[96,768]{1,0:T(8,128)(2,1)S(1)}, u32[]{:S(2)}, u32[]{:S(2)}) collective-permute-start(bf16[96,768]{1,0:T(8,128)(2,1)S(1)} %shard_map.429), channel_id=1, source_target_pairs={{0,24},{4,28},{8,16},{12,20},{16,8},{20,12},{24,0},{28,4},{1,25},{... | collective-permute-start | bytes 442376 | tf_op jit(solution)/shard_map/ppermute | solution.py:688
  147.4 1.7 %shard_map.433 = (f32[2,96,288]{2,1,0:T(8,128)}, f32[288,96]{1,0:T(8,128)}, f32[2,96,288]{2,1,0:T(8,128)}, f32[288,96]{1,0:T(8,128)}, f32[2,96,288]{2,1,0:T(8,12...) custom-call(f32[96,896]{1,0:T(8,128)S(1)} %get-tuple-element.141.refs_0_, ...), custom_call_target="tpu_custom_call" | custom-call | tf_op jit(solution)/shard_map/pallas_call | solution.py:44
  149.1 4.3 %collective-permute-done.36.refs_3_ = bf16[96,768]{1,0:T(8,128)(2,1)S(1)} collective-permute-done((bf16[96,768]{1,0:T(8,128)(2,1)S(1)}, bf16[96,768]{1,0:T(8,128)(2,1)S(1)}, u32[]{:S(2)}, u32[]{:S(2)}) %collective-permute-start.36) | collective-permute-done | bytes 147488 | tf_op jit(solution)/shard_map/ppermute | solution.py:688
  155.4 2.0 %collective-permute-start.42 = (f32[8,128]{1,0:T(8,128)S(1)}, f32[8,128]{1,0:T(8,128)S(1)}, u32[]{:S(2)}, u32[]{:S(2)}) collective-permute-start(f32[8,128]{1,0:T(8,128)S(1)} %shard_map.434.refs_0_), channel_id=1, source_target_pairs={{0,2},{1,3},{2,0},{3,1},{4,6},{5,7},{6,4},{7,5},{8,10},{9,11},{10,... | collective-permute-start | bytes 12296 | tf_op jit(solution)/shard_map/ppermute | solution.py:685
  (132 shorter events, 42.3 us)
Async XLA Ops:
  3.5 12.1 %collective-permute-start.1 = (bf16[128,1536]{1,0:T(8,128)(2,1)S(1)}, bf16[128,1536]{1,0:T(8,128)(2,1)S(1)}, u32[]{:S(2)}, u32[]{:S(2)}) collective-permute-start(bf16[128,1536]{1,0:T(8,128)(2,1)S(1)} %shard_map.413.refs_0_), channel_id=1, source_target_pairs={{0,2},{1,3},{2,0},{3,1},{4,6},{5,7},{6,4},{7,5},{8,10},{9,11},{10,... | collective-permute-start | bytes 1179656 | tf_op jit(solution)/shard_map/ppermute | solution.py:685
  7.8 12.2 %collective-permute-start.8 = (bf16[96,768]{1,0:T(8,128)(2,1)S(1)}, bf16[96,768]{1,0:T(8,128)(2,1)S(1)}, u32[]{:S(2)}, u32[]{:S(2)}) collective-permute-start(bf16[96,768]{1,0:T(8,128)(2,1)S(1)} %shard_map.414.refs_4_), channel_id=1, source_target_pairs={{0,24},{4,28},{8,16},{12,20},{16,8},{20,12},{24,0},{28,4},{1,25},{... | collective-permute-start | bytes 442376 | tf_op jit(solution)/shard_map/ppermute | solution.py:688
  11.5 26.6 %collective-permute-start = (bf16[128,1536]{1,0:T(8,128)(2,1)S(1)}, bf16[128,1536]{1,0:T(8,128)(2,1)S(1)}, u32[]{:S(2)}, u32[]{:S(2)}) collective-permute-start(bf16[128,1536]{1,0:T(8,128)(2,1)S(1)} %shard_map.413.refs_0_), channel_id=1, source_target_pairs={{0,1},{1,0},{2,3},{3,2},{4,5},{5,4},{6,7},{7,6},{8,9},{9,8},{10,11... | collective-permute-start | bytes 1179656 | tf_op jit(solution)/shard_map/ppermute | solution.py:685
  15.6 22.5 %collective-permute-start.2 = (bf16[128,1536]{1,0:T(8,128)(2,1)S(1)}, bf16[128,1536]{1,0:T(8,128)(2,1)S(1)}, u32[]{:S(2)}, u32[]{:S(2)}) collective-permute-start(bf16[128,1536]{1,0:T(8,128)(2,1)S(1)} %collective-permute-done.1.refs_2_), channel_id=1, source_target_pairs={{0,1},{1,0},{2,3},{3,2},{4,5},{5,4},{6,7},{7,6},{8,9},{9,8},{10,11... | collective-permute-start | bytes 1179656 | tf_op jit(solution)/shard_map/ppermute | solution.py:685
  15.6 10.6 %collective-permute-start.6 = (bf16[96,768]{1,0:T(8,128)(2,1)S(1)}, bf16[96,768]{1,0:T(8,128)(2,1)S(1)}, u32[]{:S(2)}, u32[]{:S(2)}) collective-permute-start(bf16[96,768]{1,0:T(8,128)(2,1)S(1)} %shard_map.414.refs_4_), channel_id=1, source_target_pairs={{0,16},{4,20},{8,24},{12,28},{16,0},{20,4},{24,8},{28,12},{1,17},{... | collective-permute-start | bytes 442376 | tf_op jit(solution)/shard_map/ppermute | solution.py:688
  18.5 9.4 %collective-permute-start.4 = (bf16[96,768]{1,0:T(8,128)(2,1)S(1)}, bf16[96,768]{1,0:T(8,128)(2,1)S(1)}, u32[]{:S(2)}, u32[]{:S(2)}) collective-permute-start(bf16[96,768]{1,0:T(8,128)(2,1)S(1)} %shard_map.414.refs_4_), channel_id=1, source_target_pairs={{0,8},{4,12},{8,0},{12,4},{16,24},{20,28},{24,16},{28,20},{1,9},{5... | collective-permute-start | bytes 442376 | tf_op jit(solution)/shard_map/ppermute | solution.py:688
  20.0 8.2 %collective-permute-start.3 = (bf16[96,768]{1,0:T(8,128)(2,1)S(1)}, bf16[96,768]{1,0:T(8,128)(2,1)S(1)}, u32[]{:S(2)}, u32[]{:S(2)}) collective-permute-start(bf16[96,768]{1,0:T(8,128)(2,1)S(1)} %shard_map.414.refs_4_), channel_id=1, source_target_pairs={{0,4},{4,0},{8,12},{12,8},{16,20},{20,16},{24,28},{28,24},{1,5},{5... | collective-permute-start | bytes 442376 | tf_op jit(solution)/shard_map/ppermute | solution.py:688
  27.8 8.3 %collective-permute-start.7 = (bf16[96,768]{1,0:T(8,128)(2,1)S(1)}, bf16[96,768]{1,0:T(8,128)(2,1)S(1)}, u32[]{:S(2)}, u32[]{:S(2)}) collective-permute-start(bf16[96,768]{1,0:T(8,128)(2,1)S(1)} %collective-permute-done.6.refs_8_), channel_id=1, source_target_pairs={{0,4},{4,0},{8,12},{12,8},{16,20},{20,16},{24,28},{28,24},{1,5},{5... | collective-permute-start | bytes 442376 | tf_op jit(solution)/shard_map/ppermute | solution.py:688
  28.3 9.8 %collective-permute-start.5 = (bf16[96,768]{1,0:T(8,128)(2,1)S(1)}, bf16[96,768]{1,0:T(8,128)(2,1)S(1)}, u32[]{:S(2)}, u32[]{:S(2)}) collective-permute-start(bf16[96,768]{1,0:T(8,128)(2,1)S(1)} %collective-permute-done.4.refs_6_), channel_id=1, source_target_pairs={{0,4},{4,0},{8,12},{12,8},{16,20},{20,16},{24,28},{28,24},{1,5},{5... | collective-permute-start | bytes 442376 | tf_op jit(solution)/shard_map/ppermute | solution.py:688
  51.8 10.8 %collective-permute-start.13 = (bf16[128,768]{1,0:T(8,128)(2,1)S(1)}, bf16[128,768]{1,0:T(8,128)(2,1)S(1)}, u32[]{:S(2)}, u32[]{:S(2)}) collective-permute-start(bf16[128,768]{1,0:T(8,128)(2,1)S(1)} %get-tuple-element.103.refs_0_), channel_id=1, source_target_pairs={{0,2},{1,3},{2,0},{3,1},{4,6},{5,7},{6,4},{7,5},{8,10},{9,11},{10,... | collective-permute-start | bytes 589832 | tf_op jit(solution)/shard_map/ppermute | solution.py:685
  53.5 9.2 %collective-permute-start.20 = (bf16[96,896]{1,0:T(8,128)(2,1)S(1)}, bf16[96,896]{1,0:T(8,128)(2,1)S(1)}, u32[]{:S(2)}, u32[]{:S(2)}) collective-permute-start(bf16[96,896]{1,0:T(8,128)(2,1)S(1)} %shard_map.418.refs_5_), channel_id=1, source_target_pairs={{0,24},{4,28},{8,16},{12,20},{16,8},{20,12},{24,0},{28,4},{1,25},{... | collective-permute-start | bytes 516104 | tf_op jit(solution)/shard_map/ppermute | solution.py:688
  57.4 13.0 %collective-permute-start.18 = (bf16[96,896]{1,0:T(8,128)(2,1)S(1)}, bf16[96,896]{1,0:T(8,128)(2,1)S(1)}, u32[]{:S(2)}, u32[]{:S(2)}) collective-permute-start(bf16[96,896]{1,0:T(8,128)(2,1)S(1)} %shard_map.418.refs_5_), channel_id=1, source_target_pairs={{0,16},{4,20},{8,24},{12,28},{16,0},{20,4},{24,8},{28,12},{1,17},{... | collective-permute-start | bytes 516104 | tf_op jit(solution)/shard_map/ppermute | solution.py:688
  57.4 14.5 %collective-permute-start.16 = (bf16[96,896]{1,0:T(8,128)(2,1)S(1)}, bf16[96,896]{1,0:T(8,128)(2,1)S(1)}, u32[]{:S(2)}, u32[]{:S(2)}) collective-permute-start(bf16[96,896]{1,0:T(8,128)(2,1)S(1)} %shard_map.418.refs_5_), channel_id=1, source_target_pairs={{0,8},{4,12},{8,0},{12,4},{16,24},{20,28},{24,16},{28,20},{1,9},{5... | collective-permute-start | bytes 516104 | tf_op jit(solution)/shard_map/ppermute | solution.py:688
  58.0 14.4 %collective-permute-start.15 = (bf16[96,896]{1,0:T(8,128)(2,1)S(1)}, bf16[96,896]{1,0:T(8,128)(2,1)S(1)}, u32[]{:S(2)}, u32[]{:S(2)}) collective-permute-start(bf16[96,896]{1,0:T(8,128)(2,1)S(1)} %shard_map.418.refs_5_), channel_id=1, source_target_pairs={{0,4},{4,0},{8,12},{12,8},{16,20},{20,16},{24,28},{28,24},{1,5},{5... | collective-permute-start | bytes 516104 | tf_op jit(solution)/shard_map/ppermute | solution.py:688
  62.7 19.7 %collective-permute-start.12 = (bf16[128,768]{1,0:T(8,128)(2,1)S(1)}, bf16[128,768]{1,0:T(8,128)(2,1)S(1)}, u32[]{:S(2)}, u32[]{:S(2)}) collective-permute-start(bf16[128,768]{1,0:T(8,128)(2,1)S(1)} %get-tuple-element.103.refs_0_), channel_id=1, source_target_pairs={{0,1},{1,0},{2,3},{3,2},{4,5},{5,4},{6,7},{7,6},{8,9},{9,8},{10,11... | collective-permute-start | bytes 589832 | tf_op jit(solution)/shard_map/ppermute | solution.py:685
  62.7 19.7 %collective-permute-start.14 = (bf16[128,768]{1,0:T(8,128)(2,1)S(1)}, bf16[128,768]{1,0:T(8,128)(2,1)S(1)}, u32[]{:S(2)}, u32[]{:S(2)}) collective-permute-start(bf16[128,768]{1,0:T(8,128)(2,1)S(1)} %collective-permute-done.13.refs_2_), channel_id=1, source_target_pairs={{0,1},{1,0},{2,3},{3,2},{4,5},{5,4},{6,7},{7,6},{8,9},{9,8},{10,11... | collective-permute-start | bytes 589832 | tf_op jit(solution)/shard_map/ppermute | solution.py:685
  70.3 7.2 %collective-permute-start.21 = (bf16[96,896]{1,0:T(8,128)(2,1)S(1)}, bf16[96,896]{1,0:T(8,128)(2,1)S(1)}, u32[]{:S(2)}, u32[]{:S(2)}) collective-permute-start(bf16[96,896]{1,0:T(8,128)(2,1)S(1)} %collective-permute-done.20.refs_11_), channel_id=1, source_target_pairs={{0,4},{4,0},{8,12},{12,8},{16,20},{20,16},{24,28},{28,24},{1,5},{5... | collective-permute-start | bytes 516104 | tf_op jit(solution)/shard_map/ppermute | solution.py:688
  71.9 8.7 %collective-permute-start.19 = (bf16[96,896]{1,0:T(8,128)(2,1)S(1)}, bf16[96,896]{1,0:T(8,128)(2,1)S(1)}, u32[]{:S(2)}, u32[]{:S(2)}) collective-permute-start(bf16[96,896]{1,0:T(8,128)(2,1)S(1)} %collective-permute-done.18.refs_9_), channel_id=1, source_target_pairs={{0,4},{4,0},{8,12},{12,8},{16,20},{20,16},{24,28},{28,24},{1,5},{5... | collective-permute-start | bytes 516104 | tf_op jit(solution)/shard_map/ppermute | solution.py:688
  72.4 10.0 %collective-permute-start.17 = (bf16[96,896]{1,0:T(8,128)(2,1)S(1)}, bf16[96,896]{1,0:T(8,128)(2,1)S(1)}, u32[]{:S(2)}, u32[]{:S(2)}) collective-permute-start(bf16[96,896]{1,0:T(8,128)(2,1)S(1)} %collective-permute-done.16.refs_7_), channel_id=1, source_target_pairs={{0,4},{4,0},{8,12},{12,8},{16,20},{20,16},{24,28},{28,24},{1,5},{5... | collective-permute-start | bytes 516104 | tf_op jit(solution)/shard_map/ppermute | solution.py:688
  101.2 30.9 %collective-permute-start.29 = (bf16[2,128,768]{2,1,0:T(8,128)(2,1)S(1)}, bf16[2,128,768]{2,1,0:T(8,128)(2,1)S(1)}, u32[]{:S(2)}, u32[]{:S(2)}) collective-permute-start(bf16[2,128,768]{2,1,0:T(8,128)(2,1)S(1)} %get-tuple-element.122), channel_id=1, source_target_pairs={{0,1},{1,0},{2,3},{3,2},{4,5},{5,4},{6,7},{7,6},{8,9},{9,8},{10,11... | collective-permute-start | bytes 1179656 | tf_op jit(solution)/shard_map/ppermute | solution.py:685
  109.7 24.4 %collective-permute-start.27 = (bf16[2,128,768]{2,1,0:T(8,128)(2,1)S(1)}, bf16[2,128,768]{2,1,0:T(8,128)(2,1)S(1)}, u32[]{:S(2)}, u32[]{:S(2)}) collective-permute-start(bf16[2,128,768]{2,1,0:T(8,128)(2,1)S(1)} %get-tuple-element.118), channel_id=1, source_target_pairs={{0,1},{1,0},{2,3},{3,2},{4,5},{5,4},{6,7},{7,6},{8,9},{9,8},{10,11... | collective-permute-start | bytes 1179656 | tf_op jit(solution)/shard_map/ppermute | solution.py:685
  111.9 10.5 %collective-permute-start.37 = (bf16[2,96,896]{2,1,0:T(8,128)(2,1)S(1)}, bf16[2,96,896]{2,1,0:T(8,128)(2,1)S(1)}, u32[]{:S(2)}, u32[]{:S(2)}) collective-permute-start(bf16[2,96,896]{2,1,0:T(8,128)(2,1)S(1)} %get-tuple-element.139), channel_id=1, source_target_pairs={{0,8},{4,12},{8,0},{12,4},{16,24},{20,28},{24,16},{28,20},{1,9},{5... | collective-permute-start | bytes 1032200 | tf_op jit(solution)/shard_map/ppermute | solution.py:688
  112.8 17.7 %collective-permute-start.38 = (bf16[2,96,896]{2,1,0:T(8,128)(2,1)S(1)}, bf16[2,96,896]{2,1,0:T(8,128)(2,1)S(1)}, u32[]{:S(2)}, u32[]{:S(2)}) collective-permute-start(bf16[2,96,896]{2,1,0:T(8,128)(2,1)S(1)} %get-tuple-element.140), channel_id=1, source_target_pairs={{0,24},{4,28},{8,16},{12,20},{16,8},{20,12},{24,0},{28,4},{1,25},{... | collective-permute-start | bytes 1032200 | tf_op jit(solution)/shard_map/ppermute | solution.py:688
  120.8 17.0 %collective-permute-start.31 = (bf16[2,96,768]{2,1,0:T(8,128)(2,1)S(1)}, bf16[2,96,768]{2,1,0:T(8,128)(2,1)S(1)}, u32[]{:S(2)}, u32[]{:S(2)}) collective-permute-start(bf16[2,96,768]{2,1,0:T(8,128)(2,1)S(1)} %get-tuple-element.128), channel_id=1, source_target_pairs={{0,4},{4,0},{8,12},{12,8},{16,20},{20,16},{24,28},{28,24},{1,5},{5... | collective-permute-start | bytes 884744 | tf_op jit(solution)/shard_map/ppermute | solution.py:688
  122.3 12.5 %collective-permute-start.33 = (bf16[1,96,768]{2,1,0:T(8,128)(2,1)S(1)}, bf16[1,96,768]{2,1,0:T(8,128)(2,1)S(1)}, u32[]{:S(2)}, u32[]{:S(2)}) collective-permute-start(bf16[1,96,768]{2,1,0:T(8,128)(2,1)S(1)} %get-tuple-element.132), channel_id=1, source_target_pairs={{0,4},{4,0},{8,12},{12,8},{16,20},{20,16},{24,28},{28,24},{1,5},{5... | collective-permute-start | bytes 442376 | tf_op jit(solution)/shard_map/ppermute | solution.py:688
  132.1 13.2 %collective-permute-start.41 = (bf16[96,896]{1,0:T(8,128)(2,1)S(1)}, bf16[96,896]{1,0:T(8,128)(2,1)S(1)}, u32[]{:S(2)}, u32[]{:S(2)}) collective-permute-start(bf16[96,896]{1,0:T(8,128)(2,1)S(1)} %shard_map.432), channel_id=1, source_target_pairs={{0,16},{4,20},{8,24},{12,28},{16,0},{20,4},{24,8},{28,12},{1,17},{... | collective-permute-start | bytes 516104 | tf_op jit(solution)/shard_map/ppermute | solution.py:688
  134.1 13.2 %collective-permute-start.39 = (bf16[96,896]{1,0:T(8,128)(2,1)S(1)}, bf16[96,896]{1,0:T(8,128)(2,1)S(1)}, u32[]{:S(2)}, u32[]{:S(2)}) collective-permute-start(bf16[96,896]{1,0:T(8,128)(2,1)S(1)} %get-tuple-element.142), channel_id=1, source_target_pairs={{0,4},{4,0},{8,12},{12,8},{16,20},{20,16},{24,28},{28,24},{1,5},{5... | collective-permute-start | bytes 516104 | tf_op jit(solution)/shard_map/ppermute | solution.py:688
  134.8 24.8 %collective-permute-start.30 = (bf16[128,768]{1,0:T(8,128)(2,1)S(1)}, bf16[128,768]{1,0:T(8,128)(2,1)S(1)}, u32[]{:S(2)}, u32[]{:S(2)}) collective-permute-start(bf16[128,768]{1,0:T(8,128)(2,1)S(1)} %get-tuple-element.124), channel_id=1, source_target_pairs={{0,2},{1,3},{2,0},{3,1},{4,6},{5,7},{6,4},{7,5},{8,10},{9,11},{10,... | collective-permute-start | bytes 589832 | tf_op jit(solution)/shard_map/ppermute | solution.py:685
  137.1 22.5 %collective-permute-start.28 = (bf16[128,768]{1,0:T(8,128)(2,1)S(1)}, bf16[128,768]{1,0:T(8,128)(2,1)S(1)}, u32[]{:S(2)}, u32[]{:S(2)}) collective-permute-start(bf16[128,768]{1,0:T(8,128)(2,1)S(1)} %get-tuple-element.120), channel_id=1, source_target_pairs={{0,2},{1,3},{2,0},{3,1},{4,6},{5,7},{6,4},{7,5},{8,10},{9,11},{10,... | collective-permute-start | bytes 589832 | tf_op jit(solution)/shard_map/ppermute | solution.py:685
  137.8 11.3 %collective-permute-start.34 = (bf16[96,768]{1,0:T(8,128)(2,1)S(1)}, bf16[96,768]{1,0:T(8,128)(2,1)S(1)}, u32[]{:S(2)}, u32[]{:S(2)}) collective-permute-start(bf16[96,768]{1,0:T(8,128)(2,1)S(1)} %shard_map.428), channel_id=1, source_target_pairs={{0,16},{4,20},{8,24},{12,28},{16,0},{20,4},{24,8},{28,12},{1,17},{... | collective-permute-start | bytes 442376 | tf_op jit(solution)/shard_map/ppermute | solution.py:688
  145.3 8.1 %collective-permute-start.36 = (bf16[96,768]{1,0:T(8,128)(2,1)S(1)}, bf16[96,768]{1,0:T(8,128)(2,1)S(1)}, u32[]{:S(2)}, u32[]{:S(2)}) collective-permute-start(bf16[96,768]{1,0:T(8,128)(2,1)S(1)} %shard_map.429), channel_id=1, source_target_pairs={{0,24},{4,28},{8,16},{12,20},{16,8},{20,12},{24,0},{28,4},{1,25},{... | collective-permute-start | bytes 442376 | tf_op jit(solution)/shard_map/ppermute | solution.py:688
  147.3 7.7 %collective-permute-start.32 = (bf16[96,768]{1,0:T(8,128)(2,1)S(1)}, bf16[96,768]{1,0:T(8,128)(2,1)S(1)}, u32[]{:S(2)}, u32[]{:S(2)}) collective-permute-start(bf16[96,768]{1,0:T(8,128)(2,1)S(1)} %get-tuple-element.130), channel_id=1, source_target_pairs={{0,8},{4,12},{8,0},{12,4},{16,24},{20,28},{24,16},{28,20},{1,9},{5... | collective-permute-start | bytes 442376 | tf_op jit(solution)/shard_map/ppermute | solution.py:688
  (37 other events, 326.6 us)
